TPU v7x, 256 devices: a whole 4x4x8 slice. The times are simulated.
256 devices in a mesh: leaf: 64 (over y, z, core), rows: 4 (over x).
Axes of the slice: x: 4, y: 4, z: 8, core: 2. Of those that a mesh axis runs over, the one named last changes fastest.
Arguments:
- mixing: bfloat16 [192, 1024, 1024], P('leaf'), may hold values from 0.04 to 2048
- emission: bfloat16 [192, 256, 1024], P('leaf'), may hold values from 0.099609375 to 10
- prior: float32 [1024], replicated, may hold values from 0.1 to 10
- parent: int32 [192], P('leaf'), may hold values from -1 to 191, as said below
- observed: int32 [192, 512], P('leaf', 'rows'), may hold values from 0 to 255
Outputs:
- pair_counts: bfloat16 [192, 1024, 1024], P('leaf', 'rows')
- emit_counts: bfloat16 [192, 256, 1024], P('leaf', None, 'rows')
Inputs may be any that keep to these rules, and one draw needn't show every extreme that they name: Nodes are numbered 3 to an index of leaf, in order. Every parent has a smaller number than its child. A node that is not the first of its index of leaf has its parent among the nodes of the same index. The first node of index d > 0 has as parent the first node of index d with its lowest set binary digit cleared. Node 0 is the root.
All inputs are finite; a program needn't handle non-finite values.
Results may differ from a plain program's by a relative error of at most 0.009.
Values may be sent and summed in bfloat16 or wider, within the bound.
A program may use at most 128 MiB of HBM per device.

v0:
```python
import jax
import jax.numpy as jnp
from jax import lax
from jax.sharding import PartitionSpec as P


def from_partner(value, axis, bit):
    mask = 2**bit
    pairs = [(source, source ^ mask) for source in range(lax.axis_size(axis))]
    return lax.ppermute(value, axis, pairs)


def in_blocks(array, dim, count):
    lengths = array.shape
    pieces = array.reshape(*lengths[:dim], count, lengths[dim] // count, *lengths[dim + 1 :])
    return jnp.moveaxis(pieces, dim, 0)


def sum_at_owner(array, axis, dim):
    count = lax.axis_size(axis)
    pieces = lax.all_to_all(in_blocks(array, dim, count), axis, 0, 0, tiled=True)
    return jnp.sum(pieces.astype(jnp.float32), axis=0)


def lift(raw, weight):
    scale = jnp.mean(raw, axis=1, keepdims=True)
    lam = (raw / scale).astype(jnp.bfloat16)
    msg = lax.dot_general(lam, weight, (((1,), (1,)), ((), ())), preferred_element_type=jnp.float32)
    return (lam, msg)


def settle(q_par, lam, msg, weight):
    ratio = (q_par / msg).astype(jnp.bfloat16)
    post = lam.astype(jnp.float32) * jnp.dot(ratio, weight, preferred_element_type=jnp.float32)
    return (ratio, post)


def per_device(mixing, emission, prior, parent, observed):
    node_count = mixing.shape[0]
    states = mixing.shape[1]
    row_count = observed.shape[1]
    values = emission.shape[1]
    levels = lax.axis_size("leaf").bit_length() - 1
    place = lax.axis_index("leaf")
    weights = (
        mixing.astype(jnp.float32) / jnp.sum(mixing.astype(jnp.float32), axis=2, keepdims=True)
    ).astype(jnp.bfloat16)
    tables = (
        emission.astype(jnp.float32) / jnp.sum(emission.astype(jnp.float32), axis=1, keepdims=True)
    ).astype(jnp.bfloat16)
    prior_share = prior / jnp.sum(prior)
    onehots = (observed[:, :, None] == jnp.arange(values, dtype=jnp.int32)[None, None, :]).astype(
        jnp.bfloat16
    )
    emits = jnp.einsum("nrv,nvk->nrk", onehots, tables, preferred_element_type=jnp.float32)
    local_parent = parent - place * node_count
    prods = jnp.ones_like(emits)
    lam_list = [None] * node_count
    msg_list = [None] * node_count
    for node in range(node_count - 1, 0, -1):
        lam, msg = lift(emits[node] * prods[node], weights[node])
        lam_list[node] = lam
        msg_list[node] = msg
        slot = local_parent[node]
        current = lax.dynamic_index_in_dim(prods, slot, 0, keepdims=False)
        prods = lax.dynamic_update_index_in_dim(prods, current * msg, slot, 0)
    block_raw = emits[0] * prods[0]
    block_weight = weights[0]
    stored = []
    for level in range(levels):
        upper = jnp.bitwise_and(place, 1 << level) != 0
        other_raw = from_partner(block_raw, "leaf", level)
        other_weight = from_partner(block_weight, "leaf", level)
        child_raw = jnp.where(upper, block_raw, other_raw)
        child_weight = jnp.where(upper, block_weight, other_weight)
        child_lam, child_msg = lift(child_raw, child_weight)
        stored.append((child_lam, child_msg, child_weight))
        block_raw = jnp.where(upper, other_raw, block_raw) * child_msg
        block_weight = jnp.where(upper, other_weight, block_weight)
    top_lam, top_msg = lift(block_raw, block_weight)
    weighted = prior_share[None, :] * top_msg
    root_share = weighted / jnp.sum(weighted, axis=1, keepdims=True)
    top_ratio, top_post = settle(root_share, top_lam, top_msg, block_weight)
    for level in reversed(range(levels)):
        upper = jnp.bitwise_and(place, 1 << level) != 0
        child_lam, child_msg, child_weight = stored[level]
        ratio, post = settle(top_post, child_lam, child_msg, child_weight)
        top_lam = jnp.where(upper, child_lam, top_lam)
        top_ratio = jnp.where(upper, ratio, top_ratio)
        top_post = jnp.where(upper, post, top_post)
    lam_list[0] = top_lam
    posts = jnp.zeros_like(emits).at[0].set(top_post)
    ratio_list = [top_ratio] + [None] * (node_count - 1)
    for node in range(1, node_count):
        q_par = lax.dynamic_index_in_dim(posts, local_parent[node], 0, keepdims=False)
        ratio, post = settle(q_par, lam_list[node], msg_list[node], weights[node])
        ratio_list[node] = ratio
        posts = posts.at[node].set(post)
    ratio_all = jnp.stack(ratio_list, axis=0)
    lam_all = jnp.stack(lam_list, axis=0)
    post_half = posts.astype(jnp.bfloat16)
    emit_part = jnp.einsum("nrv,nrk->nvk", onehots, post_half, preferred_element_type=jnp.float32)
    groups = lax.axis_size("rows")
    share = states // groups
    spread = lax.all_to_all(ratio_all, "rows", split_axis=2, concat_axis=1, tiled=True)
    flows = jnp.einsum(
        "nra,nrb->nab",
        spread,
        lax.all_gather(lam_all, "rows", axis=1, tiled=True),
        preferred_element_type=jnp.float32,
    )
    emit_sum = sum_at_owner(emit_part.astype(jnp.bfloat16), "rows", 2)
    samples = row_count * groups
    own_rows = lax.dynamic_slice_in_dim(weights, lax.axis_index("rows") * share, share, 1)
    pair_counts = (own_rows.astype(jnp.float32) * flows * (states * states / samples)).astype(
        jnp.bfloat16
    )
    emit_counts = (emit_sum * (values * states / samples)).astype(jnp.bfloat16)
    return (pair_counts, emit_counts)


def solution(mesh):
    placed = (P("leaf", None, None), P("leaf", None, None), P(), P("leaf"), P("leaf", "rows"))
    return jax.shard_map(
        per_device,
        mesh=mesh,
        in_specs=placed,
        out_specs=(P("leaf", "rows", None), P("leaf", None, "rows")),
        check_vma=False,
    )
```

profile of v0, /device:TPU:8, one launch (start us, length us, event | category | flops | bytes accessed | tf_op | source)
XLA Modules:
  0.0 503.5 jit_solution(12902194291016919670)
XLA Ops:
  7.2 3.8 convert_reduce_fusion
  11.1 0.8 copy-done.1
  11.8 2.7 fusion
  14.5 2.6 copy-done
  17.4 1.7 convert_reduce_fusion.1
  19.1 2.5 collective-permute-done.1
  21.7 1.8 broadcast_select_fusion.10
  23.5 2.0 collective-permute-start.3
  29.3 1.9 fusion.6
  31.5 0.9 copy-done.4
  32.6 3.2 bitcast_dynamic-update-slice_fusion.1
  35.8 1.2 copy-done.2
  37.0 1.1 copy.20
  38.8 1.3 fusion.44
  40.1 1.5 constant_dynamic-slice_fusion
  41.6 30.5 %collective-permute-done.3 = bf16[1024,1024]{1,0:T(8,128)(2,1)} collective-permute-done((bf16[1024,1024]{1,0:T(8,128)(2,1)S(1)}, bf16[1024,1024]{1,0:T(8,128)(2,1)}, u32[]{:S(2)}, u32[]{:S(2)}) %collective-permute-start.3) | collective-permute-done | bytes 2097184 | tf_op jit(solution)/shard_map/ppermute | solution.py:10
  72.1 1.5 broadcast_select_fusion.8
  73.7 3.3 collective-permute-start.5
  77.0 3.2 bitcast_dynamic-update-slice_fusion
  80.2 1.1 fusion.29
  81.4 1.9 collective-permute-done
  83.6 3.9 select_multiply_fusion.5
  87.5 3.3 collective-permute-start.2
  90.8 77.3 %collective-permute-done.5 = bf16[1024,1024]{1,0:T(8,128)(2,1)} collective-permute-done((bf16[1024,1024]{1,0:T(8,128)(2,1)}, bf16[1024,1024]{1,0:T(8,128)(2,1)}, u32[]{:S(2)}, u32[]{:S(2)}) %collective-permute-start.5) | collective-permute-done | bytes 2097184 | tf_op jit(solution)/shard_map/ppermute | solution.py:10
  168.1 3.1 broadcast_select_fusion.6
  171.2 6.2 %collective-permute-start.7 = (bf16[1024,1024]{1,0:T(8,128)(2,1)}, bf16[1024,1024]{1,0:T(8,128)(2,1)}, u32[]{:S(2)}, u32[]{:S(2)}) collective-permute-start(bf16[1024,1024]{1,0:T(8,128)(2,1)} %broadcast_select_fusion.6), channel_id=1, source_target_pairs={{0,32},{4,36},{8,40},{12,44},{16,48},{20,52},{24,56},{28,60},{32,0... | collective-permute-start | bytes 6291464 | tf_op jit(solution)/shard_map/ppermute | solution.py:10
  177.7 3.2 select_multiply_fusion.4
  180.9 109.8 %collective-permute-done.4 = f32[128,1024]{1,0:T(8,128)S(1)} collective-permute-done((f32[128,1024]{1,0:T(8,128)S(1)}, f32[128,1024]{1,0:T(8,128)S(1)}, u32[]{:S(2)}, u32[]{:S(2)}) %collective-permute-start.4) | collective-permute-done | bytes 524320 | tf_op jit(solution)/shard_map/ppermute | solution.py:10
  290.9 3.1 broadcast_select_fusion.4
  294.6 3.3 select_multiply_fusion.3
  297.9 3.6 collective-permute-start.6
  301.5 25.1 %collective-permute-done.6 = f32[128,1024]{1,0:T(8,128)S(1)} collective-permute-done((f32[128,1024]{1,0:T(8,128)S(1)}, f32[128,1024]{1,0:T(8,128)S(1)}, u32[]{:S(2)}, u32[]{:S(2)}) %collective-permute-start.6) | collective-permute-done | bytes 524320 | tf_op jit(solution)/shard_map/ppermute | solution.py:10
  326.9 3.4 select_multiply_fusion.2
  330.3 1.6 collective-permute-start.8
  331.9 11.0 %collective-permute-done.9 = bf16[1024,1024]{1,0:T(8,128)(2,1)} collective-permute-done((bf16[1024,1024]{1,0:T(8,128)(2,1)}, bf16[1024,1024]{1,0:T(8,128)(2,1)}, u32[]{:S(2)}, u32[]{:S(2)}) %collective-permute-start.9) | collective-permute-done | bytes 2097184 | tf_op jit(solution)/shard_map/ppermute | solution.py:10
  342.9 3.1 broadcast_select_fusion.2
  346.0 2.3 collective-permute-start.11
  348.3 5.7 %collective-permute-done.8 = f32[128,1024]{1,0:T(8,128)S(1)} collective-permute-done((f32[128,1024]{1,0:T(8,128)S(1)}, f32[128,1024]{1,0:T(8,128)S(1)}, u32[]{:S(2)}, u32[]{:S(2)}) %collective-permute-start.8) | collective-permute-done | bytes 524320 | tf_op jit(solution)/shard_map/ppermute | solution.py:10
  354.9 3.4 select_multiply_fusion.1
  358.4 2.3 collective-permute-start.10
  361.9 48.3 %collective-permute-done.10 = f32[128,1024]{1,0:T(8,128)S(1)} collective-permute-done((f32[128,1024]{1,0:T(8,128)S(1)}, f32[128,1024]{1,0:T(8,128)S(1)}, u32[]{:S(2)}, u32[]{:S(2)}) %collective-permute-start.10) | collective-permute-done | bytes 524320 | tf_op jit(solution)/shard_map/ppermute | solution.py:10
  410.6 3.4 fusion.45
  415.0 1.0 pad_maximum_fusion.1
  416.0 2.5 multiply_reduce_fusion
  418.6 2.3 divide_convert_fusion.5
  421.0 2.3 divide_convert_fusion.4
  423.3 2.3 divide_convert_fusion.3
  425.6 2.5 divide_convert_fusion.2
  428.2 2.4 divide_convert_fusion.1
  430.6 2.3 fusion.16
  433.9 2.2 select_bitcast_fusion
  436.3 0.9 copy-done.24
  437.3 1.7 fusion.10
  439.2 1.4 copy.10
  440.7 4.3 all-to-all-start
  445.0 2.1 fusion.13
  447.7 1.3 copy.17
  449.0 18.5 %all-to-all-done = bf16[3,128,1024]{1,0,2:T(4,128)(2,1)S(1)} async-done(((bf16[3,128,1024]{1,0,2:T(4,128)(2,1)}), bf16[3,128,1024]{1,0,2:T(4,128)(2,1)S(1)}, u32[]{:S(2)}, u32[]{:S(2)}) %all-to-all-start) | async-done | bytes 786464 | tf_op jit(solution)/shard_map/all_to_all | solution.py:105
  467.5 3.6 all-to-all-start.1
  471.0 1.6 copy.18
  472.7 1.6 all_to_all.19
  474.3 16.8 %all-to-all-done.1 = bf16[4,3,256,256]{3,2,1,0:T(8,128)(2,1)S(1)} async-done(((bf16[4,3,256,256]{3,2,1,0:T(8,128)(2,1)}), bf16[4,3,256,256]{3,2,1,0:T(8,128)(2,1)S(1)}, u32[]{:S(2)}, u32[]{:S(2)}) %all-to-all-start.1) | async-done | bytes 1572896 | tf_op jit(solution)/shard_map/all_to_all | solution.py:21
  491.4 0.8 multiply_convert_fusion.1
  492.2 4.5 multiply_convert_fusion
  (117 shorter events, 8.6 us)
Async XLA Ops:
  7.2 485.0 %all-gather.2.cloned.1.call-start = ((), (), s32[]{:S(2)}) async-start(), calls=%async_computation.2 | async-start | bytes 3932160 | tf_op jit(solution)/shard_map/all_gather | solution.py:109
  7.2 4.6 copy-start.1
  14.5 2.6 copy-start
  17.1 2.0 copy-start.34
  17.3 4.4 collective-permute-start.1
  19.1 10.2 %copy-start.33 = (s32[3,128]{1,0:T(4,128)S(1)}, s32[3,128]{1,0:T(4,128)}, u32[]{:S(2)}) copy-start(s32[3,128]{1,0:T(4,128)} %param.15) | copy-start | bytes 4612
  23.5 48.7 %collective-permute-start.3 = (bf16[1024,1024]{1,0:T(8,128)(2,1)S(1)}, bf16[1024,1024]{1,0:T(8,128)(2,1)}, u32[]{:S(2)}, u32[]{:S(2)}) collective-permute-start(bf16[1024,1024]{1,0:T(8,128)(2,1)S(1)} %broadcast_select_fusion.10), channel_id=1, source_target_pairs={{0,8},{4,12},{8,0},{12,4},{16,24},{20,28},{24,16},{28,20},{32,40},... | collective-permute-start | bytes 6291464 | tf_op jit(solution)/shard_map/ppermute | solution.py:10
  31.2 1.2 copy-start.4
  32.4 3.4 copy-start.22
  35.8 1.2 copy-start.2
  41.6 35.4 %copy-start.12 = (bf16[1,128,1024]{2,1,0:T(8,128)(2,1)}, bf16[1,128,1024]{2,1,0:T(8,128)(2,1)S(1)}, u32[]{:S(2)}) copy-start(bf16[1,128,1024]{2,1,0:T(8,128)(2,1)S(1)} %get-tuple-element.50) | copy-start | bytes 786436
  41.6 35.4 %copy-start.8 = (f32[3,128,1024]{2,1,0:T(8,128)S(1)}, f32[3,128,1024]{2,1,0:T(8,128)}, u32[]{:S(2)}) copy-start(f32[3,128,1024]{2,1,0:T(8,128)} %copy.20) | copy-start | bytes 4718596
  73.7 94.4 %collective-permute-start.5 = (bf16[1024,1024]{1,0:T(8,128)(2,1)}, bf16[1024,1024]{1,0:T(8,128)(2,1)}, u32[]{:S(2)}, u32[]{:S(2)}) collective-permute-start(bf16[1024,1024]{1,0:T(8,128)(2,1)} %broadcast_select_fusion.8), channel_id=1, source_target_pairs={{0,16},{4,20},{8,24},{12,28},{16,0},{20,4},{24,8},{28,12},{32,48},... | collective-permute-start | bytes 6291464 | tf_op jit(solution)/shard_map/ppermute | solution.py:10
  81.3 2.0 collective-permute-start
  83.6 4.0 copy-start.9
  87.5 89.9 %collective-permute-start.2 = (f32[128,1024]{1,0:T(8,128)S(1)}, f32[128,1024]{1,0:T(8,128)S(1)}, u32[]{:S(2)}, u32[]{:S(2)}) collective-permute-start(f32[128,1024]{1,0:T(8,128)S(1)} %get-tuple-element.57), channel_id=1, source_target_pairs={{0,8},{4,12},{8,0},{12,4},{16,24},{20,28},{24,16},{28,20},{32,40},... | collective-permute-start | bytes 1572872 | tf_op jit(solution)/shard_map/ppermute | solution.py:10
  171.2 119.7 %collective-permute-start.7 = (bf16[1024,1024]{1,0:T(8,128)(2,1)}, bf16[1024,1024]{1,0:T(8,128)(2,1)}, u32[]{:S(2)}, u32[]{:S(2)}) collective-permute-start(bf16[1024,1024]{1,0:T(8,128)(2,1)} %broadcast_select_fusion.6), channel_id=1, source_target_pairs={{0,32},{4,36},{8,40},{12,44},{16,48},{20,52},{24,56},{28,60},{32,0... | collective-permute-start | bytes 6291464 | tf_op jit(solution)/shard_map/ppermute | solution.py:10
  180.9 109.8 %collective-permute-start.4 = (f32[128,1024]{1,0:T(8,128)S(1)}, f32[128,1024]{1,0:T(8,128)S(1)}, u32[]{:S(2)}, u32[]{:S(2)}) collective-permute-start(f32[128,1024]{1,0:T(8,128)S(1)} %get-tuple-element.59), channel_id=1, source_target_pairs={{0,16},{4,20},{8,24},{12,28},{16,0},{20,4},{24,8},{28,12},{32,48},... | collective-permute-start | bytes 1572872 | tf_op jit(solution)/shard_map/ppermute | solution.py:10
  294.0 48.8 %collective-permute-start.9 = (bf16[1024,1024]{1,0:T(8,128)(2,1)}, bf16[1024,1024]{1,0:T(8,128)(2,1)}, u32[]{:S(2)}, u32[]{:S(2)}) collective-permute-start(bf16[1024,1024]{1,0:T(8,128)(2,1)} %broadcast_select_fusion.4), channel_id=1, source_target_pairs={{0,64},{4,68},{8,72},{12,76},{16,80},{20,84},{24,88},{28,92},{32,9... | collective-permute-start | bytes 6291464 | tf_op jit(solution)/shard_map/ppermute | solution.py:10
  294.6 3.3 copy-start.5
  297.9 28.7 %collective-permute-start.6 = (f32[128,1024]{1,0:T(8,128)S(1)}, f32[128,1024]{1,0:T(8,128)S(1)}, u32[]{:S(2)}, u32[]{:S(2)}) collective-permute-start(f32[128,1024]{1,0:T(8,128)S(1)} %get-tuple-element.61), channel_id=1, source_target_pairs={{0,32},{4,36},{8,40},{12,44},{16,48},{20,52},{24,56},{28,60},{32,0... | collective-permute-start | bytes 1572872 | tf_op jit(solution)/shard_map/ppermute | solution.py:10
  326.9 3.4 copy-start.14
  330.3 23.7 %collective-permute-start.8 = (f32[128,1024]{1,0:T(8,128)S(1)}, f32[128,1024]{1,0:T(8,128)S(1)}, u32[]{:S(2)}, u32[]{:S(2)}) collective-permute-start(f32[128,1024]{1,0:T(8,128)S(1)} %get-tuple-element.63), channel_id=1, source_target_pairs={{0,64},{4,68},{8,72},{12,76},{16,80},{20,84},{24,88},{28,92},{32,9... | collective-permute-start | bytes 1572872 | tf_op jit(solution)/shard_map/ppermute | solution.py:10
  346.0 64.6 %collective-permute-start.11 = (bf16[1024,1024]{1,0:T(8,128)(2,1)}, bf16[1024,1024]{1,0:T(8,128)(2,1)}, u32[]{:S(2)}, u32[]{:S(2)}) collective-permute-start(bf16[1024,1024]{1,0:T(8,128)(2,1)} %broadcast_select_fusion.2), channel_id=1, source_target_pairs={{0,128},{4,132},{8,136},{12,140},{16,144},{20,148},{24,152},{28,15... | collective-permute-start | bytes 6291464 | tf_op jit(solution)/shard_map/ppermute | solution.py:10
  354.0 0.8 copy-start.3
  354.9 3.4 copy-start.17
  354.9 5.7 %copy-start.32 = (f32[1024]{0:T(1024)S(1)}, f32[1024]{0:T(1024)}, u32[]{:S(2)}) copy-start(f32[1024]{0:T(1024)} %param.13) | copy-start | bytes 12292
  358.4 51.9 %collective-permute-start.10 = (f32[128,1024]{1,0:T(8,128)S(1)}, f32[128,1024]{1,0:T(8,128)S(1)}, u32[]{:S(2)}, u32[]{:S(2)}) collective-permute-start(f32[128,1024]{1,0:T(8,128)S(1)} %get-tuple-element.65), channel_id=1, source_target_pairs={{0,128},{4,132},{8,136},{12,140},{16,144},{20,148},{24,152},{28,15... | collective-permute-start | bytes 1572872 | tf_op jit(solution)/shard_map/ppermute | solution.py:10
  410.5 3.5 copy-start.20
  410.5 3.5 copy-start.6
  410.5 3.5 copy-start.10
  410.5 3.5 copy-start.15
  410.5 3.5 copy-start.18
  413.9 0.9 copy-start.13
  413.9 1.0 copy-start.23
  416.0 2.5 copy-start.27
  418.6 2.4 copy-start.21
  418.6 2.4 copy-start.31
  420.9 2.3 copy-start.19
  421.0 2.3 copy-start.30
  423.3 2.3 copy-start.16
  423.3 2.3 copy-start.29
  425.6 2.5 copy-start.7
  425.6 2.5 copy-start.28
  428.2 5.5 %slice-start = ((s8[6291456]{0:T(1024)(128)(4,1)}), s8[4194304]{0:T(1024)(128)(4,1)S(1)}, s32[]{:S(2)}) async-start(s8[6291456]{0:T(1024)(128)(4,1)} %bitcast.126), calls=%async_computation.3 | async-start | bytes 8388608
  430.6 2.3 copy-start.26
  430.6 3.0 slice-start.1
  432.9 1.0 copy-start.11
  436.1 1.1 copy-start.24
  437.3 1.8 copy-start.25
  440.7 26.8 %all-to-all-start = ((bf16[3,128,1024]{1,0,2:T(4,128)(2,1)}), bf16[3,128,1024]{1,0,2:T(4,128)(2,1)S(1)}, u32[]{:S(2)}, u32[]{:S(2)}) async-start(bf16[3,128,1024]{1,0,2:T(4,128)(2,1)} %copy.10), calls=%async_computation | async-start | bytes 2097152 | tf_op jit(solution)/shard_map/all_to_all | solution.py:105
  467.5 23.7 %all-to-all-start.1 = ((bf16[4,3,256,256]{3,2,1,0:T(8,128)(2,1)}), bf16[4,3,256,256]{3,2,1,0:T(8,128)(2,1)S(1)}, u32[]{:S(2)}, u32[]{:S(2)}) async-start(bf16[4,3,256,256]{3,2,1,0:T(8,128)(2,1)} %bitcast.124), calls=%async_computation.1 | async-start | bytes 3145728 | tf_op jit(solution)/shard_map/all_to_all | solution.py:21
Sparse Core Ops, SparseCore 0:
  416.1 48.4 all-gather.1
where the time goes:
time: 505 us; the launch traced here: 504 us
  waiting for transfers between devices  347 us (69%)
  matrix products  56.8 us (11%)
  starting transfers between devices  33.1 us (7%)
  other arithmetic  31.1 us (6%)
  between operations  18.7 us (4%)
  local copies, waits for them, and re-layouts  16.4 us (3%)
    ppermute x12, waiting for transfers between devices, from_partner(): return lax.ppermute(value, axis, pairs)  312 us
    dot_general x9, matrix products, lift(): lax.dot_general(lam, weight, (((1,), (1,)), ((), ())), preferred_element_...  29.7 us
    ppermute x12, starting transfers between devices, from_partner(): return lax.ppermute(value, axis, pairs)  25.2 us
    dot_general x9, matrix products, settle(): jnp.dot(ratio, weight, preferred_element_type=jnp.float32)  20.2 us
    all_to_all x1, waiting for transfers between devices, per_device(): lax.all_to_all(ratio_all, 'rows', split_axis=2, concat_axis=1, tiled=True)  18.5 us
    all_to_all x1, waiting for transfers between devices, sum_at_owner(): lax.all_to_all(in_blocks(array, dim, count), axis, 0, 0, tiled=True)  16.8 us
    select_n x5, other arithmetic, per_device(): block_weight = jnp.where(upper, other_weight, block_weight)  12.7 us
  transfers between devices with their start and end apart: 15, of which 11 were waited for; matrix products, arithmetic and copies ran while one was open for 14% of the time, Pallas kernels for 0%

commit v1 on v0

v1 whole, which is shorter than its diff:
```python
import functools

import jax
import jax.numpy as jnp
from jax import lax
from jax.experimental import pallas as pl
from jax.experimental.pallas import tpu as pltpu
from jax.sharding import PartitionSpec as P

F32 = jnp.float32
BF16 = jnp.bfloat16
CHUNKS = 4
NB = 256


def dot_nt(a, b):
    return lax.dot_general(a, b, (((1,), (1,)), ((), ())), preferred_element_type=F32)


def dot_nn(a, b):
    return lax.dot_general(a, b, (((1,), (0,)), ((), ())), preferred_element_type=F32)


def dot_tn(a, b):
    return lax.dot_general(a, b, (((0,), (0,)), ((), ())), preferred_element_type=F32)


def kernel(
    levels,
    groups,
    mixing,
    emission,
    prior,
    parent,
    observed,
    pair_out,
    emit_out,
    A,
    em,
    lam_all,
    upart,
    m2,
    msg_in,
    m_out,
    macc,
    inv_row,
    q_in,
    h0,
    q0f,
    q1f,
    qb,
    hs0,
    qs,
    ginv,
    obs_all,
    oht,
    pair_v,
    emit_v,
    load_sem,
    up_send,
    up_recv,
    dn_send,
    dn_recv,
    ag_send,
    ag_recv,
    hx_send,
    hx_recv,
    q0_send,
    q0_recv,
    qx_send,
    qx_recv,
    ob_send,
    ob_recv,
    out_sem,
):
    K = A.shape[1]
    V = em.shape[1]
    R = upart.shape[0]
    Ks = K // groups
    C = CHUNKS
    S = R // C
    pair_scale = float(K * K // (R * groups))
    emit_scale = float(V * K // (R * groups))

    d = lax.axis_index("leaf")
    r = lax.axis_index("rows")
    lvl = jnp.int32(0)
    low = jnp.int32(1)
    for j in range(levels):
        zero = jnp.where(d % (2 ** (j + 1)) == 0, 1, 0)
        lvl = lvl + zero
        low = low + zero * (2**j)
    is_root = lvl == levels
    up_dev = jnp.where(is_root, d, d - low)
    own = pl.multiple_of(r * R, R)
    mine = pl.multiple_of(r * Ks, Ks)

    def peer(k):
        return lax.rem(r + k, groups)

    order = (2, 1, 0)
    loads = {}
    for n, g in enumerate(order):
        loads["e", g] = pltpu.make_async_copy(emission.at[g], em.at[g], load_sem.at[2 * n])
        loads["m", g] = pltpu.make_async_copy(mixing.at[g], A.at[g], load_sem.at[2 * n + 1])
        loads["e", g].start()
        loads["m", g].start()

    barrier = pltpu.get_barrier_semaphore()

    def greet(leaf, rows):
        pl.semaphore_signal(
            barrier,
            inc=1,
            device_id={"leaf": leaf, "rows": rows},
            device_id_type=pl.DeviceIdType.MESH,
        )

    @pl.when(jnp.logical_not(is_root))
    def _():
        greet(up_dev, r)

    def greet_child(j, step):
        greet(d + step, r)
        return step * 2

    lax.fori_loop(0, lvl, greet_child, jnp.int32(1))
    for k in range(1, groups):
        greet(d, peer(k))

    def arrived(ref, sem):
        pltpu.make_async_remote_copy(
            src_ref=ref,
            dst_ref=ref,
            send_sem=sem,
            recv_sem=sem,
            device_id={"leaf": d, "rows": peer(1)},
            device_id_type=pl.DeviceIdType.MESH,
        ).wait_recv()

    def up_copy(i):
        rows = pl.ds(pl.multiple_of(i * S, S), S)
        return pltpu.make_async_remote_copy(
            src_ref=m_out.at[rows],
            dst_ref=msg_in.at[jnp.minimum(lvl, levels - 1), rows],
            send_sem=up_send.at[i],
            recv_sem=up_recv.at[jnp.minimum(lvl, levels - 1), i],
            device_id={"leaf": up_dev, "rows": r},
            device_id_type=pl.DeviceIdType.MESH,
        )

    def wait_up(j, i):
        rows = pl.ds(pl.multiple_of(i * S, S), S)
        arrived(msg_in.at[j, rows], up_recv.at[j, i])

    def dn_copy(j, step, i):
        rows = pl.ds(pl.multiple_of(i * S, S), S)
        return pltpu.make_async_remote_copy(
            src_ref=qb.at[0, rows],
            dst_ref=q_in.at[rows],
            send_sem=dn_send.at[j, i],
            recv_sem=dn_recv.at[i],
            device_id={"leaf": d + step, "rows": r},
            device_id_type=pl.DeviceIdType.MESH,
        )

    def wait_dn(i):
        rows = pl.ds(pl.multiple_of(i * S, S), S)
        arrived(q_in.at[rows], dn_recv.at[i])

    def ag_copy(g, k):
        return pltpu.make_async_remote_copy(
            src_ref=lam_all.at[g, pl.ds(own, R)],
            dst_ref=lam_all.at[g, pl.ds(own, R)],
            send_sem=ag_send.at[g, k - 1],
            recv_sem=ag_recv.at[g, k - 1],
            device_id={"leaf": d, "rows": peer(k)},
            device_id_type=pl.DeviceIdType.MESH,
        )

    def ag_wait(g):
        for k in range(1, groups):
            src = pl.multiple_of(lax.rem(r + groups - k, groups) * R, R)
            arrived(lam_all.at[g, pl.ds(src, R)], ag_recv.at[g, k - 1])

    def slice_copy(src, dst, send_sem, recv_sem, k, row, count):
        to = peer(k)
        cols = pl.ds(pl.multiple_of(to * Ks, Ks), Ks)
        return pltpu.make_async_remote_copy(
            src_ref=src.at[pl.ds(row, count), cols],
            dst_ref=dst.at[pl.ds(pl.multiple_of(own + row, count), count)],
            send_sem=send_sem,
            recv_sem=recv_sem,
            device_id={"leaf": d, "rows": to},
            device_id_type=pl.DeviceIdType.MESH,
        )

    def slice_wait(dst, recv_sem, k, row, count):
        src = lax.rem(r + groups - k, groups) * R
        arrived(dst.at[pl.ds(pl.multiple_of(src + row, count), count)], recv_sem)

    def ob_copy(k):
        return pltpu.make_async_remote_copy(
            src_ref=observed,
            dst_ref=obs_all.at[r],
            send_sem=ob_send.at[k - 1],
            recv_sem=ob_recv.at[k - 1],
            device_id={"leaf": d, "rows": peer(k)},
            device_id_type=pl.DeviceIdType.MESH,
        )

    chain = parent[2] == d * 3 + 1
    ones = jnp.ones((16, K), BF16)
    values = lax.broadcasted_iota(jnp.int32, (V, R), 0)

    def emitted(g):
        loads["e", g].wait()
        hot = jnp.where(values == observed[g : g + 1, :], 1.0, 0.0).astype(BF16)
        table = em[g]
        column = jnp.sum(table.astype(F32), axis=0, keepdims=True)
        return dot_tn(hot, table) * (1.0 / column)

    def scaled(u):
        return (u / jnp.mean(u, axis=1, keepdims=True)).astype(BF16)

    def lift_local(g, u):
        lam = scaled(u)
        lam_all[g, pl.ds(own, R), :] = lam
        left = jnp.concatenate([lam, ones], axis=0)
        loads["m", g].wait()
        parts = []
        for n in range(K // NB):
            cols = slice(n * NB, (n + 1) * NB)
            acc = dot_nt(left, A[g, cols, :])
            macc[g, :, cols] = acc[:R]
            parts.append(acc[:R] * (1.0 / acc[R : R + 1]))
        return parts

    parts = lift_local(2, emitted(2))
    for n, part in enumerate(parts):
        m2[:, n * NB : (n + 1) * NB] = part
    parts = lift_local(1, emitted(1) * jnp.where(chain, m2[...], 1.0))
    for n, part in enumerate(parts):
        cols = slice(n * NB, (n + 1) * NB)
        upart[:, cols] = part * jnp.where(chain, 1.0, m2[:, cols])
    upart[...] = upart[...] * emitted(0)
    loads["m", 0].wait()

    pl.semaphore_wait(barrier, lvl + (groups - 1) + jnp.where(is_root, 0, 1))

    def aux():
        for k in range(1, groups):
            ob_copy(k).start()
        for g in (2, 1):
            for k in range(1, groups):
                ag_copy(g, k).start()
        for g in (2, 1):
            macc[g] = 1.0 / macc[g]

    @pl.when(lvl > 0)
    def _():
        aux()

    def early_child(j, carry):
        for i in range(C):
            wait_up(j, i)
        upart[...] = upart[...] * msg_in[j].astype(F32)
        return carry

    lax.fori_loop(0, lvl - 1, early_child, 0)

    def up(i):
        rows = pl.ds(pl.multiple_of(i * S, S), S)

        @pl.when(lvl > 0)
        def _():
            wait_up(lvl - 1, i)
            upart[rows, :] = upart[rows, :] * msg_in[lvl - 1, rows, :].astype(F32)

        lam = scaled(upart[rows, :])
        lam_all[0, pl.ds(pl.multiple_of(own + i * S, S), S), :] = lam
        acc = dot_nt(jnp.concatenate([lam, ones], axis=0), A[0])
        inverse = 1.0 / acc[S : S + 1]
        m_out[rows, :] = (acc[:S] * inverse).astype(BF16)

        @pl.when(jnp.logical_not(is_root))
        def _():
            up_copy(i).start()

        inv_row[0:1, :] = inverse
        macc[0, rows, :] = jnp.where(is_root, acc[:S], 1.0 / acc[:S])

    def down(i):
        row = pl.multiple_of(i * S, S)
        rows = pl.ds(row, S)

        @pl.when(is_root)
        def _():
            weight = (prior[...] / jnp.sum(prior[...], axis=1, keepdims=True)) * inv_row[0:1, :]
            total = jnp.sum(weight * macc[0, rows, :], axis=1, keepdims=True)
            h0[rows, :] = (weight / total).astype(BF16)

        @pl.when(jnp.logical_not(is_root))
        def _():
            wait_dn(i)
            h0[rows, :] = (q_in[rows, :].astype(F32) * macc[0, rows, :]).astype(BF16)

        h = h0[rows, :]
        lam = lam_all[0, pl.ds(pl.multiple_of(own + row, S), S), :].astype(F32)
        q = lam * dot_nn(h, A[0])
        qb[0, rows, :] = q.astype(BF16)

        def send_child(n, step):
            dn_copy(lvl - 1 - n, step, i).start()
            return step // 2

        lax.fori_loop(0, lvl, send_child, low // 2)
        for k in range(1, groups):
            slice_copy(h0, hs0, hx_send.at[k - 1, i], hx_recv.at[k - 1, i], k, row, S).start()
        for k in range(1, groups):
            slice_copy(
                qb.at[0], qs.at[0], q0_send.at[k - 1, i], q0_recv.at[k - 1, i], k, row, S
            ).start()
        q0f[rows, :] = q
        there = pl.ds(pl.multiple_of(own + row, S), S)
        hs0[there, :] = h0[rows, pl.ds(mine, Ks)]
        qs[0, there, :] = qb[0, rows, pl.ds(mine, Ks)]

    def middle():
        for k in range(1, groups):
            src = lax.rem(r + groups - k, groups)
            arrived(obs_all.at[src], ob_recv.at[k - 1])
        obs_all[r] = observed[...]
        for g in range(3):
            for n in range(groups):
                oht[g, :, n * R : (n + 1) * R] = jnp.where(
                    values == obs_all[n, g : g + 1, :], 1.0, 0.0
                ).astype(BF16)
        for g in (2, 1):
            ag_wait(g)
            block = A[g, pl.ds(mine, Ks), :]
            for n in range(groups):
                part = slice(n * R, (n + 1) * R)
                ginv[g - 1, part, :] = 1.0 / dot_nt(lam_all[g, part, :], block)

    early_mid = lvl <= 1
    mid_step = jnp.where(early_mid, C, 2 * C)

    def step(s, carry):
        is_mid = s == mid_step
        t = s - jnp.where(s > mid_step, 1, 0)
        is_up = jnp.where(is_root, t % 2 == 0, t < C)
        is_up = jnp.logical_and(is_up, jnp.logical_not(is_mid))
        is_down = jnp.logical_not(jnp.logical_or(is_up, is_mid))
        i = jnp.where(is_root, t // 2, t % C)
        i = jnp.where(is_mid, 0, i)

        @pl.when(is_up)
        def _():
            up(i)

            @pl.when(i == C - 1)
            def _():
                for k in range(1, groups):
                    ag_copy(0, k).start()

                @pl.when(lvl == 0)
                def _():
                    aux()

        @pl.when(is_mid)
        def _():
            middle()

        @pl.when(is_down)
        def _():
            down(i)

        return carry

    lax.fori_loop(0, 2 * C + 1, step, 0)

    def settle_local(g, q_par):
        h = (q_par * macc[g]).astype(BF16)
        lam = lam_all[g, pl.ds(own, R), :]
        out = []
        for n in range(K // NB):
            cols = slice(n * NB, (n + 1) * NB)
            q = lam[:, cols].astype(F32) * dot_nn(h, A[g, :, cols])
            qb[g, :, cols] = q.astype(BF16)
            if g == 1:
                q1f[:, cols] = q
        for k in range(1, groups):
            slice_copy(
                qb.at[g], qs.at[g], qx_send.at[g - 1, k - 1], qx_recv.at[g - 1, k - 1], k, 0, R
            ).start()
        qs[g, pl.ds(own, R), :] = qb[g, :, pl.ds(mine, Ks)]

    settle_local(1, q0f[...])
    settle_local(2, jnp.where(chain, q1f[...], q0f[...]))

    def finish(g, h):
        cells = dot_tn(h, lam_all[g])
        raw = A[g, pl.ds(mine, Ks), :].astype(F32)
        pair_v[g] = (raw * cells * pair_scale).astype(BF16)
        pltpu.make_async_copy(pair_v.at[g], pair_out.at[g], out_sem.at[g]).start()

    def tally(g):
        emit_v[g] = (dot_nn(oht[g], qs[g]) * emit_scale).astype(BF16)
        pltpu.make_async_copy(emit_v.at[g], emit_out.at[g], out_sem.at[3 + g]).start()

    ag_wait(0)
    for k in range(1, groups):
        for i in range(C):
            slice_wait(hs0, hx_recv.at[k - 1, i], k, i * S, S)
    finish(0, hs0[...])
    for k in range(1, groups):
        for i in range(C):
            slice_wait(qs.at[0], q0_recv.at[k - 1, i], k, i * S, S)
    h1 = (qs[0].astype(F32) * ginv[0]).astype(BF16)
    finish(1, h1)
    tally(0)
    for k in range(1, groups):
        slice_wait(qs.at[1], qx_recv.at[0, k - 1], k, 0, R)
    h2 = (jnp.where(chain, qs[1].astype(F32), qs[0].astype(F32)) * ginv[1]).astype(BF16)
    finish(2, h2)
    tally(1)
    for k in range(1, groups):
        slice_wait(qs.at[2], qx_recv.at[1, k - 1], k, 0, R)
    tally(2)

    @pl.when(jnp.logical_not(is_root))
    def _():
        for i in range(C):
            up_copy(i).wait_send()

    def drain_child(n, step):
        for i in range(C):
            dn_copy(lvl - 1 - n, step, i).wait_send()
        return step // 2

    lax.fori_loop(0, lvl, drain_child, low // 2)
    for k in range(1, groups):
        ob_copy(k).wait_send()
        for g in range(3):
            ag_copy(g, k).wait_send()
        for i in range(C):
            slice_copy(
                h0, hs0, hx_send.at[k - 1, i], hx_recv.at[k - 1, i], k, i * S, S
            ).wait_send()
            slice_copy(
                qb.at[0], qs.at[0], q0_send.at[k - 1, i], q0_recv.at[k - 1, i], k, i * S, S
            ).wait_send()
        for g in (1, 2):
            slice_copy(
                qb.at[g], qs.at[g], qx_send.at[g - 1, k - 1], qx_recv.at[g - 1, k - 1], k, 0, R
            ).wait_send()
    for g in range(3):
        pltpu.make_async_copy(pair_v.at[g], pair_out.at[g], out_sem.at[g]).wait()
        pltpu.make_async_copy(emit_v.at[g], emit_out.at[g], out_sem.at[3 + g]).wait()


def per_device(levels, groups, mixing, emission, prior, parent, observed):
    nodes, K, _ = mixing.shape
    V = emission.shape[1]
    R = observed.shape[1]
    Ks = K // groups
    T = groups * R
    C = CHUNKS
    dma = pltpu.SemaphoreType.DMA
    vmem = pltpu.VMEM
    return pl.pallas_call(
        functools.partial(kernel, levels, groups),
        out_shape=(
            jax.ShapeDtypeStruct((nodes, Ks, K), BF16),
            jax.ShapeDtypeStruct((nodes, V, Ks), BF16),
        ),
        in_specs=[
            pl.BlockSpec(memory_space=pl.ANY),
            pl.BlockSpec(memory_space=pl.ANY),
            pl.BlockSpec(memory_space=pltpu.VMEM),
            pl.BlockSpec(memory_space=pltpu.SMEM),
            pl.BlockSpec(memory_space=pltpu.VMEM),
        ],
        out_specs=(pl.BlockSpec(memory_space=pl.ANY), pl.BlockSpec(memory_space=pl.ANY)),
        scratch_shapes=[
            vmem((nodes, K, K), BF16),
            vmem((nodes, V, K), BF16),
            vmem((nodes, T, K), BF16),
            vmem((R, K), F32),
            vmem((R, K), F32),
            vmem((levels, R, K), BF16),
            vmem((R, K), BF16),
            vmem((nodes, R, K), F32),
            vmem((8, K), F32),
            vmem((R, K), BF16),
            vmem((R, K), BF16),
            vmem((R, K), F32),
            vmem((R, K), F32),
            vmem((nodes, R, K), BF16),
            vmem((T, Ks), BF16),
            vmem((nodes, T, Ks), BF16),
            vmem((2, T, Ks), F32),
            vmem((groups, nodes, R), jnp.int32),
            vmem((nodes, V, T), BF16),
            vmem((nodes, Ks, K), BF16),
            vmem((nodes, V, Ks), BF16),
            dma((6,)),
            dma((C,)),
            dma((levels, C)),
            dma((levels, C)),
            dma((C,)),
            dma((3, groups - 1)),
            dma((3, groups - 1)),
            dma((groups - 1, C)),
            dma((groups - 1, C)),
            dma((groups - 1, C)),
            dma((groups - 1, C)),
            dma((2, groups - 1)),
            dma((2, groups - 1)),
            dma((groups - 1,)),
            dma((groups - 1,)),
            dma((6,)),
        ],
        compiler_params=pltpu.CompilerParams(
            collective_id=0, has_side_effects=True, vmem_limit_bytes=60 * 1024 * 1024
        ),
        name="tree_pass",
    )(mixing, emission, prior.reshape(1, K), parent, observed)


def solution(mesh):
    levels = mesh.shape["leaf"].bit_length() - 1
    groups = mesh.shape["rows"]
    placed = (P("leaf", None, None), P("leaf", None, None), P(), P("leaf"), P("leaf", "rows"))
    return jax.shard_map(
        functools.partial(per_device, levels, groups),
        mesh=mesh,
        in_specs=placed,
        out_specs=(P("leaf", "rows", None), P("leaf", None, "rows")),
        check_vma=False,
    )
```

time: 505 us -> 77.8 us (0.15)
  the two profiles are of different devices: /device:TPU:8 before, /device:TPU:249 now
where the time goes in v1:
time: 77.8 us; the launch traced here: 77.6 us
  Pallas kernels  73.5 us (94%)
  local copies, waits for them, and re-layouts  3.47 us (4%)
    pallas_call x1, Pallas kernels, per_device(): pl.pallas_call(functools.partial(kernel, levels, groups), out_shape=(jax....  73.5 us
    unnamed x4, local copies, waits for them, and re-layouts  3.47 us

profile of v1, /device:TPU:249, one launch (start us, length us, event | category | flops | bytes accessed | tf_op | source)
XLA Modules:
  0.0 77.6 jit_solution(13935659078966972383)
XLA Ops:
  0.6 73.5 %tree_pass.1 = (bf16[3,256,1024]{2,1,0:T(8,128)(2,1)}, bf16[3,256,256]{2,1,0:T(8,128)(2,1)}) custom-call(bf16[3,1024,1024]{2,1,0:T(8,128)(2,1)} %mixing.1, bf16[3,256,1024]{2,1,0:T(8,128)(2,1)} %emission.1, f32[1,1024]{1,0:T(1,128)} %bitcast.1, s32[3]{0:T(128)} %parent.1, s32[3,128]{1,0:T(4,128)} %observed.1), custom_call_target="tpu_custom_call" | custom-call | tf_op jit(solution)/shard_map/tree_pass/pallas_call | solution.py:472
  74.2 0.0 copy-start
  74.2 2.7 %copy.9 = bf16[3,256,1024]{2,1,0:T(8,128)(2,1)} copy(bf16[3,256,1024]{2,1,0:T(8,128)(2,1)} %get-tuple-element.4) | data formatting | bytes 3145728
  76.9 0.0 copy-done
  76.9 0.7 copy.10
Async XLA Ops:
  74.2 2.7 %copy-start = (bf16[3,256,256]{2,1,0:T(8,128)(2,1)S(1)}, bf16[3,256,256]{2,1,0:T(8,128)(2,1)}, u32[]{:S(2)}) copy-start(bf16[3,256,256]{2,1,0:T(8,128)(2,1)} %get-tuple-element.5) | copy-start | bytes 1179652

commit v2 on v1

v2 whole, which is shorter than its diff:
```python
import functools

import jax
import jax.numpy as jnp
from jax import lax
from jax.experimental import pallas as pl
from jax.experimental.pallas import tpu as pltpu
from jax.sharding import PartitionSpec as P

F32 = jnp.float32
BF16 = jnp.bfloat16
CHUNKS = 4
HALVES = 2
COST_FLOPS = 10**9
COST_BYTES = 10**7
VMEM_BYTES = 48_000_000
NB = 256


def dot_nt(a, b):
    return lax.dot_general(a, b, (((1,), (1,)), ((), ())), preferred_element_type=F32)


def dot_nn(a, b):
    return lax.dot_general(a, b, (((1,), (0,)), ((), ())), preferred_element_type=F32)


def dot_tn(a, b):
    return lax.dot_general(a, b, (((0,), (0,)), ((), ())), preferred_element_type=F32)


def kernel(
    levels,
    groups,
    mixing,
    emission,
    prior,
    parent,
    observed,
    pair_v,
    emit_v,
    A,
    A0T,
    em,
    lam_all,
    upart,
    m2,
    msg_in,
    m_out,
    macc,
    inv_row,
    q_in,
    h0,
    q0f,
    q1f,
    qb,
    qp,
    qs,
    relay,
    ginv,
    obs_all,
    oht,
    load_sem,
    up_send,
    up_recv,
    dn_send,
    dn_recv,
    ag_send,
    ag_recv,
    q0_send,
    q0_recv,
    qx_send,
    qx_recv,
    rl_send,
    rl_recv,
    qp_send,
    qp_recv,
    tp_send,
    tp_recv,
    ob_send,
    ob_recv,
):
    K = A.shape[1]
    V = em.shape[1]
    R = upart.shape[0]
    Ks = K // groups
    C = CHUNKS
    S = R // C
    H = HALVES
    W = K // H
    pair_scale = float(K * K // (R * groups))
    emit_scale = float(V * K // (R * groups))
    pieces = [(i, h) for i in range(C) for h in range(H)]

    d = lax.axis_index("leaf")
    r = lax.axis_index("rows")
    lvl = jnp.int32(0)
    low = jnp.int32(1)
    for j in range(levels):
        zero = jnp.where(d % (2 ** (j + 1)) == 0, 1, 0)
        lvl = lvl + zero
        low = low + zero * (2**j)
    is_root = lvl == levels
    odd = d % 2
    up_dev = jnp.where(is_root, d, d - low)
    slot = jnp.minimum(lvl, levels - 1)
    own = pl.multiple_of(r * R, R)
    mine = pl.multiple_of(r * Ks, Ks)

    def peer(k):
        return lax.rem(r + k, groups)

    def block(k):
        return pl.ds(pl.multiple_of(lax.rem(r + groups - k, groups) * R, R), R)

    loads = {}
    for n, g in enumerate((2, 1, 0)):
        loads["e", g] = pltpu.make_async_copy(emission.at[g], em.at[g], load_sem.at[2 * n])
        loads["m", g] = pltpu.make_async_copy(mixing.at[g], A.at[g], load_sem.at[2 * n + 1])
        loads["e", g].start()
        loads["m", g].start()

    barrier = pltpu.get_barrier_semaphore()

    def greet(leaf, rows):
        pl.semaphore_signal(
            barrier,
            inc=1,
            device_id={"leaf": leaf, "rows": rows},
            device_id_type=pl.DeviceIdType.MESH,
        )

    @pl.when(jnp.logical_not(is_root))
    def _():
        greet(up_dev, r)

    def greet_child(j, step):
        greet(d + step, r)
        return step * 2

    lax.fori_loop(0, lvl, greet_child, jnp.int32(1))
    for k in range(1, groups):
        greet(d, peer(k))

    def remote(src, dst, send_sem, recv_sem, leaf, rows):
        return pltpu.make_async_remote_copy(
            src_ref=src,
            dst_ref=dst,
            send_sem=send_sem,
            recv_sem=recv_sem,
            device_id={"leaf": leaf, "rows": rows},
            device_id_type=pl.DeviceIdType.MESH,
        )

    def arrived(ref, sem):
        remote(ref, ref, sem, sem, d, peer(1)).wait_recv()

    def spot(i, h):
        return pl.ds(pl.multiple_of(i * S, S), S), pl.ds(h * W, W)

    def up_copy(i, h):
        rows, cols = spot(i, h)
        return remote(
            m_out.at[rows, cols],
            msg_in.at[slot, rows, cols],
            up_send.at[i, h],
            up_recv.at[slot, i, h],
            up_dev,
            r,
        )

    def wait_up(j, i):
        for h in range(H):
            rows, cols = spot(i, h)
            arrived(msg_in.at[j, rows, cols], up_recv.at[j, i, h])

    def dn_copy(j, step, i, h):
        rows, cols = spot(i, h)
        return remote(
            qb.at[0, rows, cols],
            q_in.at[rows, cols],
            dn_send.at[j, i, h],
            dn_recv.at[i, h],
            d + step,
            r,
        )

    def wait_dn(i):
        for h in range(H):
            rows, cols = spot(i, h)
            arrived(q_in.at[rows, cols], dn_recv.at[i, h])

    near = jnp.where(odd == 0, 1, groups - 1)
    far = groups - near

    def ag_copy(g, k):
        there = pl.ds(own, R)
        return remote(
            lam_all.at[g, there],
            lam_all.at[g, there],
            ag_send.at[g, k - 1],
            ag_recv.at[g, k - 1],
            d,
            peer(k),
        )

    def ag_forward(g):
        there = block(near)
        return remote(
            lam_all.at[g, there],
            lam_all.at[g, there],
            ag_send.at[g, 1],
            ag_recv.at[g, 1],
            d,
            peer(near),
        )

    def ag_relay(g):
        arrived(lam_all.at[g, block(near)], ag_recv.at[g, near - 1])
        ag_forward(g).start()

    def ag_wait(g):
        arrived(lam_all.at[g, block(far)], ag_recv.at[g, far - 1])
        arrived(lam_all.at[g, block(2)], ag_recv.at[g, 1])

    def columns(k):
        return pl.ds(pl.multiple_of(peer(k) * Ks, Ks), Ks)

    def q0_copy(k, i):
        row = pl.multiple_of(i * S, S)
        return remote(
            qb.at[0, pl.ds(row, S), columns(k)],
            qs.at[0, pl.ds(pl.multiple_of(own + row, S), S)],
            q0_send.at[k - 1, i],
            q0_recv.at[k - 1, i],
            d,
            peer(k),
        )

    half = R // 2

    def part_of(k, n):
        start = lax.rem(r + groups - k, groups) * R + n * half
        return pl.ds(pl.multiple_of(start, half), half)

    def qx_copy(g, n, k):
        return remote(
            qb.at[g, pl.ds(n * half, half), columns(k)],
            qs.at[g, part_of(0, n)],
            qx_send.at[g - 1, n, k - 1],
            qx_recv.at[g - 1, n, k - 1],
            d,
            peer(k),
        )

    def qx_first(g):
        return remote(
            qb.at[g, pl.ds(0, half), columns(2)],
            relay.at[g - 1],
            qx_send.at[g - 1, 0, 1],
            rl_recv.at[g - 1],
            d,
            peer(groups - 1),
        )

    def qx_second(g):
        return remote(
            relay.at[g - 1],
            qs.at[g, part_of(groups - 1, 0)],
            rl_send.at[g - 1],
            qx_recv.at[g - 1, 0, 1],
            d,
            peer(groups - 1),
        )

    def pass_on(g):
        arrived(relay.at[g - 1], rl_recv.at[g - 1])
        qx_second(g).start()

    def qx_wait(g):
        for n in range(2):
            for k in range(1, groups):
                arrived(qs.at[g, part_of(k, n)], qx_recv.at[g - 1, n, k - 1])

    def qp_copy(j, step):
        return remote(qs.at[0], qp, qp_send.at[j], qp_recv.at[0], d + step, r)

    def tp_copy(k):
        return remote(
            q_in.at[:, columns(k)],
            qp.at[pl.ds(own, R)],
            tp_send.at[k - 1],
            tp_recv.at[k - 1],
            d,
            peer(k),
        )

    def ob_copy(k):
        return remote(observed, obs_all.at[r], ob_send.at[k - 1], ob_recv.at[k - 1], d, peer(k))

    chain = parent[2] == d * 3 + 1
    ones = jnp.ones((16, K), BF16)
    values = lax.broadcasted_iota(jnp.int32, (V, R), 0)

    def emitted(g):
        loads["e", g].wait()
        hot = jnp.where(values == observed[g : g + 1, :], 1.0, 0.0).astype(BF16)
        table = em[g]
        column = jnp.sum(table.astype(F32), axis=0, keepdims=True)
        return dot_tn(hot, table) * (1.0 / column)

    def scaled(u):
        return (u * (1.0 / jnp.mean(u, axis=1, keepdims=True))).astype(BF16)

    def lift_local(g, u):
        lam = scaled(u)
        lam_all[g, pl.ds(own, R), :] = lam
        left = jnp.concatenate([lam, ones], axis=0)
        if g > 0:
            loads["m", g].wait()
        parts = []
        for n in range(K // NB):
            cols = slice(n * NB, (n + 1) * NB)
            acc = dot_nt(left, A[g, cols, :])
            macc[g, :, cols] = acc[:R]
            parts.append(acc[:R] * (1.0 / acc[R : R + 1]))
        return parts

    parts = lift_local(2, emitted(2))
    for n, part in enumerate(parts):
        m2[:, n * NB : (n + 1) * NB] = part
    parts = lift_local(1, emitted(1) * jnp.where(chain, m2[...], 1.0))
    for n, part in enumerate(parts):
        cols = slice(n * NB, (n + 1) * NB)
        upart[:, cols] = part * jnp.where(chain, 1.0, m2[:, cols])
    upart[...] = upart[...] * emitted(0)
    loads["m", 0].wait()

    pl.semaphore_wait(barrier, lvl + (groups - 1) + jnp.where(is_root, 0, 1))

    def aux():
        for k in range(1, groups):
            ob_copy(k).start()
        for g in (2, 1):
            ag_copy(g, 1).start()
            ag_copy(g, groups - 1).start()
        for g in (2, 1):
            macc[g] = 1.0 / macc[g]

    @pl.when(lvl == 0)
    def _():
        for n, part in enumerate(lift_local(0, upart[...])):
            m_out[:, n * NB : (n + 1) * NB] = part.astype(BF16)
        for i, h in pieces:
            up_copy(i, h).start()
        ag_copy(0, 1).start()
        ag_copy(0, groups - 1).start()
        aux()
        macc[0] = 1.0 / macc[0]

    @pl.when(lvl > 0)
    def _():
        aux()
        for b in range(K // NB):
            A0T[:, b * NB : (b + 1) * NB] = A[0, b * NB : (b + 1) * NB, :].T

    def early_child(j, carry):
        for i in range(C):
            wait_up(j, i)
        upart[...] = upart[...] * msg_in[j].astype(F32)
        return carry

    lax.fori_loop(0, lvl - 1, early_child, 0)

    def up(i):
        rows = pl.ds(pl.multiple_of(i * S, S), S)

        wait_up(lvl - 1, i)
        lam = scaled(upart[rows, :] * msg_in[lvl - 1, rows, :].astype(F32))
        left = jnp.concatenate([lam, ones], axis=0)
        for h in range(H):
            cols = slice(h * W, (h + 1) * W)
            acc = dot_nn(left, A0T[:, cols])
            inverse = 1.0 / acc[S : S + 1]
            m_out[rows, cols] = (acc[:S] * inverse).astype(BF16)

            @pl.when(jnp.logical_not(is_root))
            def _():
                up_copy(i, h).start()

            inv_row[0:1, cols] = inverse
            macc[0, rows, cols] = jnp.where(is_root, acc[:S], 1.0 / acc[:S])
        lam_all[0, pl.ds(pl.multiple_of(own + i * S, S), S), :] = lam

    at_once = [(0, lvl > 1)]
    if levels > 4:
        at_once.append((3, lvl > 4))
    if levels > 5:
        at_once.append((4, lvl > 5))
    if levels > 3:
        at_once.append((2, lvl > 3))
    if levels > 2:
        at_once.append((1, lvl == 3))

    def down(i):
        row = pl.multiple_of(i * S, S)
        rows = pl.ds(row, S)

        @pl.when(is_root)
        def _():
            weight = (prior[...] / jnp.sum(prior[...], axis=1, keepdims=True)) * inv_row[0:1, :]
            joint = weight * macc[0, rows, :]
            part = 1.0 / jnp.sum(joint, axis=1, keepdims=True)
            h0[rows, :] = (weight * part).astype(BF16)
            q_in[rows, :] = (joint * part).astype(BF16)
            macc[0, rows, :] = 1.0 / macc[0, rows, :]

        @pl.when(jnp.logical_not(is_root))
        def _():
            wait_dn(i)
            h0[rows, :] = (q_in[rows, :].astype(F32) * macc[0, rows, :]).astype(BF16)

        left = h0[rows, :]
        for h in range(H):
            cols = slice(h * W, (h + 1) * W)
            lam = lam_all[0, pl.ds(pl.multiple_of(own + row, S), S), cols].astype(F32)
            q = lam * dot_nn(left, A[0, :, cols])
            qb[0, rows, cols] = q.astype(BF16)

            @pl.when(lvl > 0)
            def _():
                dn_copy(lvl - 1, low // 2, i, h).start()

            for j, test in at_once:

                @pl.when(test)
                def _(j=j):
                    dn_copy(j, 2**j, i, h).start()

            q0f[rows, cols] = q
        for k in range(1, groups):
            q0_copy(k, i).start()
        qs[0, pl.ds(pl.multiple_of(own + row, S), S), :] = qb[0, rows, pl.ds(mine, Ks)]

    def middle():
        for k in range(1, groups):
            src = lax.rem(r + groups - k, groups)
            arrived(obs_all.at[src], ob_recv.at[k - 1])
        obs_all[r] = observed[...]
        for g in range(3):
            for n in range(groups):
                oht[g, :, n * R : (n + 1) * R] = jnp.where(
                    values == obs_all[n, g : g + 1, :], 1.0, 0.0
                ).astype(BF16)
        for g in (2, 1, 0):
            ag_wait(g)
            share = A[g, pl.ds(mine, Ks), :]
            for n in range(groups):
                part = slice(n * R, (n + 1) * R)
                ginv[g, part, :] = 1.0 / dot_nt(lam_all[g, part, :], share)

    def settle_local(g, n, q_par):
        part = slice(n * half, (n + 1) * half)
        h = (q_par * macc[g, part, :]).astype(BF16)
        for b in range(K // NB):
            cols = slice(b * NB, (b + 1) * NB)
            lam = lam_all[g, part_of(0, n), cols].astype(F32)
            q = lam * dot_nn(h, A[g, :, cols])
            qb[g, part, cols] = q.astype(BF16)
            if g == 1:
                q1f[part, cols] = q
        for k in (1, groups - 1):
            qx_copy(g, n, k).start()
        if n == 0:
            qx_first(g).start()
        else:
            qx_copy(g, n, 2).start()
        qs[g, part_of(0, n), :] = qb[g, part, pl.ds(mine, Ks)]

    def settle_both(n):
        part = slice(n * half, (n + 1) * half)
        settle_local(1, n, q0f[part, :])
        settle_local(2, n, jnp.where(chain, q1f[part, :], q0f[part, :]))

    def step(s, carry):
        is_up = jnp.where(is_root, s % 2 == 0, s < C)
        i = jnp.where(is_root, s // 2, s % C)

        @pl.when(jnp.logical_and(s == C, jnp.logical_not(is_root)))
        def _():
            ag_relay(2)
            ag_relay(1)
            ag_relay(0)

            @pl.when(lvl <= 1)
            def _():
                middle()

        @pl.when(jnp.logical_and(is_up, lvl > 0))
        def _():
            up(i)

            @pl.when(i == C - 1)
            def _():
                ag_copy(0, 1).start()
                ag_copy(0, groups - 1).start()

        @pl.when(jnp.logical_not(is_up))
        def _():
            down(i)

            @pl.when(i == C // 2 - 1)
            def _():
                settle_both(0)

        return carry

    lax.fori_loop(0, 2 * C, step, 0)

    def all_sends(j, step, begin):
        for i, h in pieces:
            copy = dn_copy(j, step, i, h)
            if begin:
                copy.start()
            else:
                copy.wait_send()

    if levels > 3:

        @pl.when(lvl > 3)
        def _():
            all_sends(1, 2, True)

    @pl.when(lvl > 1)
    def _():
        for k in range(1, groups):
            tp_copy(k).start()
        qp[pl.ds(own, R), :] = q_in[:, pl.ds(mine, Ks)]

    @pl.when(is_root)
    def _():
        ag_relay(2)
        ag_relay(1)
        ag_relay(0)

    @pl.when(lvl > 1)
    def _():
        middle()

    settle_both(1)
    pass_on(1)
    pass_on(2)

    @pl.when(jnp.logical_not(is_root))
    def _():
        for i, h in pieces:
            up_copy(i, h).wait_send()

    for k in range(1, groups):
        ob_copy(k).wait_send()
    for g in range(3):
        ag_copy(g, 1).wait_send()
        ag_copy(g, groups - 1).wait_send()
        ag_forward(g).wait_send()

    @pl.when(lvl > 0)
    def _():
        all_sends(lvl - 1, low // 2, False)

    for j, test in at_once:

        @pl.when(test)
        def _(j=j):
            all_sends(j, 2**j, False)


    def finish(g, q_par):
        h = (q_par * ginv[g]).astype(BF16)
        cells = dot_tn(h, lam_all[g])
        raw = A[g, pl.ds(mine, Ks), :].astype(F32)
        pair_v[g] = (raw * cells * pair_scale).astype(BF16)

    def tally(g):
        emit_v[g] = (dot_nn(oht[g], qs[g]) * emit_scale).astype(BF16)

    for k in range(1, groups):
        for i in range(C):
            row = pl.multiple_of(lax.rem(r + groups - k, groups) * R + i * S, S)
            arrived(qs.at[0, pl.ds(row, S)], q0_recv.at[k - 1, i])
            q0_copy(k, i).wait_send()

    for j in (0, 1):

        @pl.when(lvl > j)
        def _():
            qp_copy(j, 2**j).start()

    tally(0)
    finish(1, qs[0].astype(F32))
    qx_wait(1)
    finish(2, jnp.where(chain, qs[1].astype(F32), qs[0].astype(F32)))
    tally(1)

    @pl.when(lvl > 1)
    def _():
        for k in range(1, groups):
            arrived(qp.at[block(k)], tp_recv.at[k - 1])

    @pl.when(lvl <= 1)
    def _():
        arrived(qp, qp_recv.at[0])

    finish(0, qp[...].astype(F32))
    qx_wait(2)
    tally(2)

    if levels > 3:

        @pl.when(lvl > 3)
        def _():
            all_sends(1, 2, False)

    @pl.when(lvl > 1)
    def _():
        for k in range(1, groups):
            tp_copy(k).wait_send()

    for j in (0, 1):

        @pl.when(lvl > j)
        def _():
            qp_copy(j, 2**j).wait_send()

    for g in (1, 2):
        for n in range(2):
            for k in range(1, groups):
                qx_copy(g, n, k).wait_send()
        qx_second(g).wait_send()


def store(pair_v, emit_v, pair_out, emit_out, sem):
    first = pltpu.make_async_copy(pair_v, pair_out, sem.at[0])
    second = pltpu.make_async_copy(emit_v, emit_out, sem.at[1])
    first.start()
    second.start()
    first.wait()
    second.wait()


def per_device(levels, groups, mixing, emission, prior, parent, observed):
    nodes, K, _ = mixing.shape
    V = emission.shape[1]
    R = observed.shape[1]
    Ks = K // groups
    T = groups * R
    C = CHUNKS
    H = HALVES
    dma = pltpu.SemaphoreType.DMA
    vmem = pltpu.VMEM
    in_vmem = pl.BlockSpec(memory_space=pltpu.VMEM)
    in_place = pl.BlockSpec(memory_space=pltpu.HBM)
    results = (
        jax.ShapeDtypeStruct((nodes, Ks, K), BF16),
        jax.ShapeDtypeStruct((nodes, V, Ks), BF16),
    )
    hold = functools.partial(pltpu.with_memory_space_constraint, memory_space=pltpu.HBM)
    pair_v, emit_v = pl.pallas_call(
        functools.partial(kernel, levels, groups),
        out_shape=results,
        in_specs=[
            in_place,
            in_place,
            in_vmem,
            pl.BlockSpec(memory_space=pltpu.SMEM),
            in_vmem,
        ],
        out_specs=(in_vmem, in_vmem),
        scratch_shapes=[
            vmem((nodes, K, K), BF16),
            vmem((K, K), BF16),
            vmem((nodes, V, K), BF16),
            vmem((nodes, T, K), BF16),
            vmem((R, K), F32),
            vmem((R, K), F32),
            vmem((levels, R, K), BF16),
            vmem((R, K), BF16),
            vmem((nodes, R, K), F32),
            vmem((8, K), F32),
            vmem((R, K), BF16),
            vmem((R, K), BF16),
            vmem((R, K), F32),
            vmem((R, K), F32),
            vmem((nodes, R, K), BF16),
            vmem((T, Ks), BF16),
            vmem((nodes, T, Ks), BF16),
            vmem((2, R // 2, Ks), BF16),
            vmem((nodes, T, Ks), F32),
            vmem((groups, nodes, R), jnp.int32),
            vmem((nodes, V, T), BF16),
            dma((6,)),
            dma((C, H)),
            dma((levels, C, H)),
            dma((levels, C, H)),
            dma((C, H)),
            dma((3, groups - 1)),
            dma((3, groups - 1)),
            dma((groups - 1, C)),
            dma((groups - 1, C)),
            dma((2, 2, groups - 1)),
            dma((2, 2, groups - 1)),
            dma((2,)),
            dma((2,)),
            dma((2,)),
            dma((1,)),
            dma((groups - 1,)),
            dma((groups - 1,)),
            dma((groups - 1,)),
            dma((groups - 1,)),
        ],
        compiler_params=pltpu.CompilerParams(
            collective_id=0, has_side_effects=True, vmem_limit_bytes=VMEM_BYTES
        ),
        cost_estimate=pl.CostEstimate(flops=COST_FLOPS, bytes_accessed=COST_BYTES, transcendentals=0),
        name="tree_pass",
    )(hold(mixing), hold(emission), hold(prior.reshape(1, K)), hold(parent), hold(observed))
    return pl.pallas_call(
        store,
        out_shape=results,
        in_specs=[in_vmem, in_vmem],
        out_specs=(in_place, in_place),
        scratch_shapes=[dma((2,))],
        compiler_params=pltpu.CompilerParams(vmem_limit_bytes=1024 * 1024),
        name="store_counts",
    )(pair_v, emit_v)


def solution(mesh):
    levels = mesh.shape["leaf"].bit_length() - 1
    groups = mesh.shape["rows"]
    placed = (P("leaf", None, None), P("leaf", None, None), P(), P("leaf"), P("leaf", "rows"))
    return jax.shard_map(
        functools.partial(per_device, levels, groups),
        mesh=mesh,
        in_specs=placed,
        out_specs=(P("leaf", "rows", None), P("leaf", None, "rows")),
        check_vma=False,
    )
```

time: 77.8 us -> 70.7 us (0.909)
  Pallas kernels: 73.5 us -> 69.4 us
  local copies, waits for them, and re-layouts: 3.47 us -> 0 us
    pallas_call x1 -> x2, Pallas kernels: 73.5 us -> 69.4 us  [the longest x1 68.1 us: per_device(): pl.pallas_call(functools.partial(kernel, levels, groups), out_shape=resul...]
    unnamed x4 -> x0, local copies, waits for them, and re-layouts: 3.47 us -> none
where the time goes in v2:
time: 70.7 us; the launch traced here: 70.1 us
  Pallas kernels  69.4 us (98%)
    pallas_call x1, Pallas kernels, per_device(): pl.pallas_call(functools.partial(kernel, levels, groups), out_shape=resul...  68.1 us

profile of v2, /device:TPU:249, one launch (start us, length us, event | category | flops | bytes accessed | tf_op | source)
XLA Modules:
  0.0 70.1 jit_solution(6574785726301546972)
XLA Ops:
  0.6 68.1 %tree_pass.1 = (bf16[3,256,1024]{2,1,0:T(8,128)(2,1)S(1)}, bf16[3,256,256]{2,1,0:T(8,128)(2,1)S(1)}) custom-call(bf16[3,1024,1024]{2,1,0:T(8,128)(2,1)} %mixing.1, bf16[3,256,1024]{2,1,0:T(8,128)(2,1)} %emission.1, f32[1,1024]{1,0:T(1,128)} %bitcast.1, s32[3]{0:T(128)} %parent.1, s32[3,128]{1,0:T(4,128)} %observed.1), custom_call_target="tpu_custom_call" | custom-call | flops 1000000000 | bytes 10000000 | tf_op jit(solution)/shard_map/tree_pass/pallas_call | solution.py:667
  68.8 1.3 %store_counts.1 = (bf16[3,256,1024]{2,1,0:T(8,128)(2,1)}, bf16[3,256,256]{2,1,0:T(8,128)(2,1)}) custom-call(bf16[3,256,1024]{2,1,0:T(8,128)(2,1)S(1)} %get-tuple-element.4.pair_v, bf16[3,256,256]{2,1,0:T(8,128)(2,1)S(1)} %get-tuple-element.5.emit_v), custom_call_target="tpu_custom_call" | custom-call | tf_op jit(solution)/shard_map/store_counts/pallas_call | solution.py:726

commit v3 on v2

--- a/solution.py
+++ b/solution.py
@@ -9,8 +9,7 @@
 
 F32 = jnp.float32
 BF16 = jnp.bfloat16
-CHUNKS = 4
-HALVES = 2
+CHUNKS = 8
 COST_FLOPS = 10**9
 COST_BYTES = 10**7
 VMEM_BYTES = 48_000_000
@@ -50,7 +49,6 @@
     macc,
     inv_row,
     q_in,
-    h0,
     q0f,
     q1f,
     qb,
@@ -63,6 +61,7 @@
     load_sem,
     up_send,
     up_recv,
+    early_recv,
     dn_send,
     dn_recv,
     ag_send,
@@ -86,11 +85,8 @@
     Ks = K // groups
     C = CHUNKS
     S = R // C
-    H = HALVES
-    W = K // H
     pair_scale = float(K * K // (R * groups))
     emit_scale = float(V * K // (R * groups))
-    pieces = [(i, h) for i in range(C) for h in range(H)]
 
     d = lax.axis_index("leaf")
     r = lax.axis_index("rows")
@@ -101,6 +97,9 @@
         lvl = lvl + zero
         low = low + zero * (2**j)
     is_root = lvl == levels
+    last = jnp.where(lvl == levels - 1, 1, 0)
+    for j in range(levels - 1):
+        last = last + jnp.where(lvl == j, (d // (2 ** (j + 1))) % 2, 0)
     odd = d % 2
     up_dev = jnp.where(is_root, d, d - low)
     slot = jnp.minimum(lvl, levels - 1)
@@ -155,40 +154,30 @@
     def arrived(ref, sem):
         remote(ref, ref, sem, sem, d, peer(1)).wait_recv()
 
-    def spot(i, h):
-        return pl.ds(pl.multiple_of(i * S, S), S), pl.ds(h * W, W)
-
-    def up_copy(i, h):
-        rows, cols = spot(i, h)
-        return remote(
-            m_out.at[rows, cols],
-            msg_in.at[slot, rows, cols],
-            up_send.at[i, h],
-            up_recv.at[slot, i, h],
-            up_dev,
-            r,
-        )
-
-    def wait_up(j, i):
-        for h in range(H):
-            rows, cols = spot(i, h)
-            arrived(msg_in.at[j, rows, cols], up_recv.at[j, i, h])
-
-    def dn_copy(j, step, i, h):
-        rows, cols = spot(i, h)
-        return remote(
-            qb.at[0, rows, cols],
-            q_in.at[rows, cols],
-            dn_send.at[j, i, h],
-            dn_recv.at[i, h],
-            d + step,
-            r,
-        )
-
-    def wait_dn(i):
-        for h in range(H):
-            rows, cols = spot(i, h)
-            arrived(q_in.at[rows, cols], dn_recv.at[i, h])
+    def sent(ref, sem):
+        remote(ref, ref, sem, sem, d, peer(1)).wait_send()
+
+    def chunk(i):
+        return pl.ds(pl.multiple_of(i * S, S), S)
+
+    def up_start(i):
+        def go(recv_sem):
+            remote(
+                m_out.at[chunk(i)], msg_in.at[slot, chunk(i)], up_send.at[0], recv_sem, up_dev, r
+            ).start()
+
+        @pl.when(last == 1)
+        def _():
+            go(up_recv.at[i])
+
+        @pl.when(last == 0)
+        def _():
+            go(early_recv.at[slot])
+
+    def dn_start(j, step, i):
+        remote(
+            qb.at[0, chunk(i)], q_in.at[chunk(i)], dn_send.at[j], dn_recv.at[i], d + step, r
+        ).start()
 
     near = jnp.where(odd == 0, 1, groups - 1)
     far = groups - near
@@ -198,7 +187,7 @@
         return remote(
             lam_all.at[g, there],
             lam_all.at[g, there],
-            ag_send.at[g, k - 1],
+            ag_send.at[g],
             ag_recv.at[g, k - 1],
             d,
             peer(k),
@@ -209,7 +198,7 @@
         return remote(
             lam_all.at[g, there],
             lam_all.at[g, there],
-            ag_send.at[g, 1],
+            ag_send.at[g],
             ag_recv.at[g, 1],
             d,
             peer(near),
@@ -226,13 +215,13 @@
     def columns(k):
         return pl.ds(pl.multiple_of(peer(k) * Ks, Ks), Ks)
 
-    def q0_copy(k, i):
+    def q0_copy(k, i, m):
         row = pl.multiple_of(i * S, S)
         return remote(
-            qb.at[0, pl.ds(row, S), columns(k)],
-            qs.at[0, pl.ds(pl.multiple_of(own + row, S), S)],
-            q0_send.at[k - 1, i],
-            q0_recv.at[k - 1, i],
+            qb.at[0, pl.ds(row, m * S), columns(k)],
+            qs.at[0, pl.ds(pl.multiple_of(own + row, S), m * S)],
+            q0_send.at[0],
+            q0_recv.at[k - 1],
             d,
             peer(k),
         )
@@ -247,8 +236,8 @@
         return remote(
             qb.at[g, pl.ds(n * half, half), columns(k)],
             qs.at[g, part_of(0, n)],
-            qx_send.at[g - 1, n, k - 1],
-            qx_recv.at[g - 1, n, k - 1],
+            qx_send.at[g - 1],
+            qx_recv.at[g - 1, k - 1],
             d,
             peer(k),
         )
@@ -257,7 +246,7 @@
         return remote(
             qb.at[g, pl.ds(0, half), columns(2)],
             relay.at[g - 1],
-            qx_send.at[g - 1, 0, 1],
+            qx_send.at[g - 1],
             rl_recv.at[g - 1],
             d,
             peer(groups - 1),
@@ -267,8 +256,8 @@
         return remote(
             relay.at[g - 1],
             qs.at[g, part_of(groups - 1, 0)],
-            rl_send.at[g - 1],
-            qx_recv.at[g - 1, 0, 1],
+            rl_send.at[0],
+            qx_recv.at[g - 1, 1],
             d,
             peer(groups - 1),
         )
@@ -278,25 +267,24 @@
         qx_second(g).start()
 
     def qx_wait(g):
-        for n in range(2):
-            for k in range(1, groups):
-                arrived(qs.at[g, part_of(k, n)], qx_recv.at[g - 1, n, k - 1])
+        for k in range(1, groups):
+            arrived(qs.at[g, block(k)], qx_recv.at[g - 1, k - 1])
 
     def qp_copy(j, step):
-        return remote(qs.at[0], qp, qp_send.at[j], qp_recv.at[0], d + step, r)
+        return remote(qs.at[0], qp, qp_send.at[0], qp_recv.at[0], d + step, r)
 
     def tp_copy(k):
         return remote(
             q_in.at[:, columns(k)],
             qp.at[pl.ds(own, R)],
-            tp_send.at[k - 1],
+            tp_send.at[0],
             tp_recv.at[k - 1],
             d,
             peer(k),
         )
 
     def ob_copy(k):
-        return remote(observed, obs_all.at[r], ob_send.at[k - 1], ob_recv.at[k - 1], d, peer(k))
+        return remote(observed, obs_all.at[r], ob_send.at[0], ob_recv.at[k - 1], d, peer(k))
 
     chain = parent[2] == d * 3 + 1
     ones = jnp.ones((16, K), BF16)
@@ -351,8 +339,8 @@
     def _():
         for n, part in enumerate(lift_local(0, upart[...])):
             m_out[:, n * NB : (n + 1) * NB] = part.astype(BF16)
-        for i, h in pieces:
-            up_copy(i, h).start()
+        for i in range(C):
+            up_start(i)
         ag_copy(0, 1).start()
         ag_copy(0, groups - 1).start()
         aux()
@@ -365,82 +353,73 @@
             A0T[:, b * NB : (b + 1) * NB] = A[0, b * NB : (b + 1) * NB, :].T
 
     def early_child(j, carry):
-        for i in range(C):
-            wait_up(j, i)
+        arrived(msg_in.at[j], early_recv.at[j])
         upart[...] = upart[...] * msg_in[j].astype(F32)
         return carry
 
     lax.fori_loop(0, lvl - 1, early_child, 0)
 
-    def up(i):
-        rows = pl.ds(pl.multiple_of(i * S, S), S)
-
-        wait_up(lvl - 1, i)
+    @pl.when(is_root)
+    def _():
+        ag_relay(2)
+        ag_relay(1)
+
+    def up(i, m=1):
+        M = m * S
+        rows = pl.ds(pl.multiple_of(i * S, S), M)
+        for n in range(m):
+            arrived(msg_in.at[lvl - 1, chunk(i + n)], up_recv.at[i + n])
         lam = scaled(upart[rows, :] * msg_in[lvl - 1, rows, :].astype(F32))
-        left = jnp.concatenate([lam, ones], axis=0)
-        for h in range(H):
-            cols = slice(h * W, (h + 1) * W)
-            acc = dot_nn(left, A0T[:, cols])
-            inverse = 1.0 / acc[S : S + 1]
-            m_out[rows, cols] = (acc[:S] * inverse).astype(BF16)
-
-            @pl.when(jnp.logical_not(is_root))
-            def _():
-                up_copy(i, h).start()
-
-            inv_row[0:1, cols] = inverse
-            macc[0, rows, cols] = jnp.where(is_root, acc[:S], 1.0 / acc[:S])
-        lam_all[0, pl.ds(pl.multiple_of(own + i * S, S), S), :] = lam
+        acc = dot_nn(jnp.concatenate([lam, ones], axis=0), A0T[...])
+        inverse = 1.0 / acc[M : M + 1]
+        if m == 1:
+            m_out[rows, :] = (acc[:M] * inverse).astype(BF16)
+            up_start(i)
+            macc[0, rows, :] = 1.0 / acc[:M]
+        else:
+            inv_row[0:1, :] = inverse
+            macc[0, rows, :] = acc[:M]
+        lam_all[0, pl.ds(pl.multiple_of(own + i * S, S), M), :] = lam
 
     at_once = [(0, lvl > 1)]
     if levels > 4:
         at_once.append((3, lvl > 4))
-    if levels > 5:
-        at_once.append((4, lvl > 5))
-    if levels > 3:
-        at_once.append((2, lvl > 3))
-    if levels > 2:
-        at_once.append((1, lvl == 3))
-
-    def down(i):
+
+    def down(i, m=1):
+        M = m * S
         row = pl.multiple_of(i * S, S)
-        rows = pl.ds(row, S)
-
-        @pl.when(is_root)
-        def _():
+        rows = pl.ds(row, M)
+        if m == 1:
+            arrived(q_in.at[rows], dn_recv.at[i])
+            left = (q_in[rows, :].astype(F32) * macc[0, rows, :]).astype(BF16)
+        else:
             weight = (prior[...] / jnp.sum(prior[...], axis=1, keepdims=True)) * inv_row[0:1, :]
             joint = weight * macc[0, rows, :]
             part = 1.0 / jnp.sum(joint, axis=1, keepdims=True)
-            h0[rows, :] = (weight * part).astype(BF16)
+            left = (weight * part).astype(BF16)
             q_in[rows, :] = (joint * part).astype(BF16)
-            macc[0, rows, :] = 1.0 / macc[0, rows, :]
-
-        @pl.when(jnp.logical_not(is_root))
-        def _():
-            wait_dn(i)
-            h0[rows, :] = (q_in[rows, :].astype(F32) * macc[0, rows, :]).astype(BF16)
-
-        left = h0[rows, :]
-        for h in range(H):
-            cols = slice(h * W, (h + 1) * W)
-            lam = lam_all[0, pl.ds(pl.multiple_of(own + row, S), S), cols].astype(F32)
-            q = lam * dot_nn(left, A[0, :, cols])
-            qb[0, rows, cols] = q.astype(BF16)
+        there = pl.ds(pl.multiple_of(own + row, S), M)
+        q = lam_all[0, there, :].astype(F32) * dot_nn(left, A[0])
+        qb[0, rows, :] = q.astype(BF16)
+        for n in range(m):
 
             @pl.when(lvl > 0)
             def _():
-                dn_copy(lvl - 1, low // 2, i, h).start()
+                dn_start(lvl - 1, low // 2, i + n)
 
             for j, test in at_once:
 
                 @pl.when(test)
                 def _(j=j):
-                    dn_copy(j, 2**j, i, h).start()
-
-            q0f[rows, cols] = q
+                    dn_start(j, 2**j, i + n)
+
+        if m > 1 and levels > 5:
+            for n in range(m):
+                dn_start(4, 16, i + n)
+        q0f[rows, :] = q
         for k in range(1, groups):
-            q0_copy(k, i).start()
-        qs[0, pl.ds(pl.multiple_of(own + row, S), S), :] = qb[0, rows, pl.ds(mine, Ks)]
+            q0_copy(k, i, m).start()
+        qs[0, there, :] = qb[0, rows, pl.ds(mine, Ks)]
 
     def middle():
         for k in range(1, groups):
@@ -482,12 +461,25 @@
         settle_local(1, n, q0f[part, :])
         settle_local(2, n, jnp.where(chain, q1f[part, :], q0f[part, :]))
 
+    def gather_first():
+        ag_copy(0, 1).start()
+        ag_copy(0, groups - 1).start()
+
+    @pl.when(is_root)
+    def _():
+        up(0, C // 2)
+        down(0, C // 2)
+        up(C // 2, C // 2)
+        down(C // 2, C // 2)
+        gather_first()
+
     def step(s, carry):
-        is_up = jnp.where(is_root, s % 2 == 0, s < C)
-        i = jnp.where(is_root, s // 2, s % C)
-
-        @pl.when(jnp.logical_and(s == C, jnp.logical_not(is_root)))
+        @pl.when(s == C)
         def _():
+            @pl.when(lvl > 0)
+            def _():
+                gather_first()
+
             ag_relay(2)
             ag_relay(1)
             ag_relay(0)
@@ -496,40 +488,33 @@
             def _():
                 middle()
 
-        @pl.when(jnp.logical_and(is_up, lvl > 0))
+        @pl.when(s < C)
         def _():
-            up(i)
-
-            @pl.when(i == C - 1)
-            def _():
-                ag_copy(0, 1).start()
-                ag_copy(0, groups - 1).start()
-
-        @pl.when(jnp.logical_not(is_up))
+            up(s)
+
+        @pl.when(s >= C)
         def _():
-            down(i)
-
-            @pl.when(i == C // 2 - 1)
+            down(s - C)
+
+            @pl.when(jnp.logical_and(s == C + C // 2 - 1, lvl <= 1))
             def _():
                 settle_both(0)
 
         return carry
 
-    lax.fori_loop(0, 2 * C, step, 0)
-
-    def all_sends(j, step, begin):
-        for i, h in pieces:
-            copy = dn_copy(j, step, i, h)
-            if begin:
-                copy.start()
-            else:
-                copy.wait_send()
-
+    lax.fori_loop(jnp.where(lvl == 0, C, 0), jnp.where(is_root, 0, 2 * C), step, 0)
+
+    later = []
     if levels > 3:
-
-        @pl.when(lvl > 3)
-        def _():
-            all_sends(1, 2, True)
+        later.append((2, lvl > 3))
+    if levels > 2:
+        later.append((1, lvl > 2))
+    for j, test in later:
+
+        @pl.when(test)
+        def _(j=j):
+            for i in range(C):
+                dn_start(j, 2**j, i)
 
     @pl.when(lvl > 1)
     def _():
@@ -539,13 +524,25 @@
 
     @pl.when(is_root)
     def _():
-        ag_relay(2)
-        ag_relay(1)
         ag_relay(0)
 
     @pl.when(lvl > 1)
     def _():
+        settle_both(0)
+
+    def share():
+        for k in range(1, groups):
+            arrived(qs.at[0, block(k)], q0_recv.at[k - 1])
+        for j in (0, 1):
+
+            @pl.when(lvl > j)
+            def _():
+                qp_copy(j, 2**j).start()
+
+    @pl.when(lvl > 1)
+    def _():
         middle()
+        share()
 
     settle_both(1)
     pass_on(1)
@@ -553,26 +550,17 @@
 
     @pl.when(jnp.logical_not(is_root))
     def _():
-        for i, h in pieces:
-            up_copy(i, h).wait_send()
-
-    for k in range(1, groups):
-        ob_copy(k).wait_send()
+        sent(m_out, up_send.at[0])
+
+    sent(obs_all.at[0 : groups - 1], ob_send.at[0])
     for g in range(3):
-        ag_copy(g, 1).wait_send()
-        ag_copy(g, groups - 1).wait_send()
-        ag_forward(g).wait_send()
-
-    @pl.when(lvl > 0)
-    def _():
-        all_sends(lvl - 1, low // 2, False)
-
-    for j, test in at_once:
-
-        @pl.when(test)
-        def _(j=j):
-            all_sends(j, 2**j, False)
-
+        sent(lam_all.at[g, 0 : 3 * R], ag_send.at[g])
+
+    def sent_child(j, carry):
+        sent(qb.at[0], dn_send.at[j])
+        return carry
+
+    lax.fori_loop(0, lvl, sent_child, 0)
 
     def finish(g, q_par):
         h = (q_par * ginv[g]).astype(BF16)
@@ -583,59 +571,43 @@
     def tally(g):
         emit_v[g] = (dot_nn(oht[g], qs[g]) * emit_scale).astype(BF16)
 
-    for k in range(1, groups):
-        for i in range(C):
-            row = pl.multiple_of(lax.rem(r + groups - k, groups) * R + i * S, S)
-            arrived(qs.at[0, pl.ds(row, S)], q0_recv.at[k - 1, i])
-            q0_copy(k, i).wait_send()
-
-    for j in (0, 1):
-
-        @pl.when(lvl > j)
-        def _():
-            qp_copy(j, 2**j).start()
+    @pl.when(lvl <= 1)
+    def _():
+        share()
 
     tally(0)
     finish(1, qs[0].astype(F32))
+    @pl.when(lvl > 1)
+    def _():
+        for k in range(1, groups):
+            arrived(qp.at[block(k)], tp_recv.at[k - 1])
+
+    @pl.when(lvl <= 1)
+    def _():
+        arrived(qp, qp_recv.at[0])
+
+    finish(0, qp[...].astype(F32))
     qx_wait(1)
     finish(2, jnp.where(chain, qs[1].astype(F32), qs[0].astype(F32)))
     tally(1)
-
-    @pl.when(lvl > 1)
-    def _():
-        for k in range(1, groups):
-            arrived(qp.at[block(k)], tp_recv.at[k - 1])
-
-    @pl.when(lvl <= 1)
-    def _():
-        arrived(qp, qp_recv.at[0])
-
-    finish(0, qp[...].astype(F32))
     qx_wait(2)
     tally(2)
 
-    if levels > 3:
-
-        @pl.when(lvl > 3)
-        def _():
-            all_sends(1, 2, False)
+    three = (groups - 1) * R
 
     @pl.when(lvl > 1)
     def _():
-        for k in range(1, groups):
-            tp_copy(k).wait_send()
-
-    for j in (0, 1):
-
-        @pl.when(lvl > j)
-        def _():
-            qp_copy(j, 2**j).wait_send()
-
+        sent(qp.at[0:three], tp_send.at[0])
+        sent(qs.at[0:2], qp_send.at[0])
+
+    @pl.when(lvl == 1)
+    def _():
+        sent(qs.at[0], qp_send.at[0])
+
+    sent(qs.at[0, 0:three], q0_send.at[0])
     for g in (1, 2):
-        for n in range(2):
-            for k in range(1, groups):
-                qx_copy(g, n, k).wait_send()
-        qx_second(g).wait_send()
+        sent(qs.at[g, 0:three], qx_send.at[g - 1])
+    sent(relay, rl_send.at[0])
 
 
 def store(pair_v, emit_v, pair_out, emit_out, sem):
@@ -654,7 +626,6 @@
     Ks = K // groups
     T = groups * R
     C = CHUNKS
-    H = HALVES
     dma = pltpu.SemaphoreType.DMA
     vmem = pltpu.VMEM
     in_vmem = pl.BlockSpec(memory_space=pltpu.VMEM)
@@ -687,7 +658,6 @@
             vmem((nodes, R, K), F32),
             vmem((8, K), F32),
             vmem((R, K), BF16),
-            vmem((R, K), BF16),
             vmem((R, K), F32),
             vmem((R, K), F32),
             vmem((nodes, R, K), BF16),
@@ -698,23 +668,24 @@
             vmem((groups, nodes, R), jnp.int32),
             vmem((nodes, V, T), BF16),
             dma((6,)),
-            dma((C, H)),
-            dma((levels, C, H)),
-            dma((levels, C, H)),
-            dma((C, H)),
-            dma((3, groups - 1)),
-            dma((3, groups - 1)),
-            dma((groups - 1, C)),
-            dma((groups - 1, C)),
-            dma((2, 2, groups - 1)),
-            dma((2, 2, groups - 1)),
+            dma((1,)),
+            dma((C,)),
+            dma((levels,)),
+            dma((levels,)),
+            dma((C,)),
+            dma((nodes,)),
+            dma((nodes, groups - 1)),
+            dma((1,)),
+            dma((groups - 1,)),
             dma((2,)),
-            dma((2,)),
+            dma((2, groups - 1)),
+            dma((1,)),
             dma((2,)),
             dma((1,)),
+            dma((1,)),
+            dma((1,)),
             dma((groups - 1,)),
-            dma((groups - 1,)),
-            dma((groups - 1,)),
+            dma((1,)),
             dma((groups - 1,)),
         ],
         compiler_params=pltpu.CompilerParams(

time: 70.7 us -> 69.1 us (0.977)
  the two profiles are of different devices: /device:TPU:249 before, /device:TPU:59 now
where the time goes in v3:
time: 69.1 us; the launch traced here: 69 us
  Pallas kernels  68.3 us (99%)
    pallas_call x1, Pallas kernels, per_device(): pl.pallas_call(functools.partial(kernel, levels, groups), out_shape=resul...  67.1 us

profile of v3, /device:TPU:59, one launch (start us, length us, event | category | flops | bytes accessed | tf_op | source)
XLA Modules:
  0.0 69.0 jit_solution(12421040103934483013)
XLA Ops:
  0.6 67.1 %tree_pass.1 = (bf16[3,256,1024]{2,1,0:T(8,128)(2,1)S(1)}, bf16[3,256,256]{2,1,0:T(8,128)(2,1)S(1)}) custom-call(bf16[3,1024,1024]{2,1,0:T(8,128)(2,1)} %mixing.1, bf16[3,256,1024]{2,1,0:T(8,128)(2,1)} %emission.1, f32[1,1024]{1,0:T(1,128)} %bitcast.1, s32[3]{0:T(128)} %parent.1, s32[3,128]{1,0:T(4,128)} %observed.1), custom_call_target="tpu_custom_call" | custom-call | flops 1000000000 | bytes 10000000 | tf_op jit(solution)/shard_map/tree_pass/pallas_call | solution.py:638
  67.7 1.3 %store_counts.1 = (bf16[3,256,1024]{2,1,0:T(8,128)(2,1)}, bf16[3,256,256]{2,1,0:T(8,128)(2,1)}) custom-call(bf16[3,256,1024]{2,1,0:T(8,128)(2,1)S(1)} %get-tuple-element.4.pair_v, bf16[3,256,256]{2,1,0:T(8,128)(2,1)S(1)} %get-tuple-element.5.emit_v), custom_call_target="tpu_custom_call" | custom-call | tf_op jit(solution)/shard_map/store_counts/pallas_call | solution.py:697

commit v4 on v3

--- a/solution.py
+++ b/solution.py
@@ -116,8 +116,9 @@
     for n, g in enumerate((2, 1, 0)):
         loads["e", g] = pltpu.make_async_copy(emission.at[g], em.at[g], load_sem.at[2 * n])
         loads["m", g] = pltpu.make_async_copy(mixing.at[g], A.at[g], load_sem.at[2 * n + 1])
-        loads["e", g].start()
-        loads["m", g].start()
+    for kind in ("e", "m"):
+        for g in (2, 1, 0):
+            loads[kind, g].start()
 
     barrier = pltpu.get_barrier_semaphore()
 
@@ -304,8 +305,7 @@
         lam = scaled(u)
         lam_all[g, pl.ds(own, R), :] = lam
         left = jnp.concatenate([lam, ones], axis=0)
-        if g > 0:
-            loads["m", g].wait()
+        loads["m", g].wait()
         parts = []
         for n in range(K // NB):
             cols = slice(n * NB, (n + 1) * NB)
@@ -314,14 +314,16 @@
             parts.append(acc[:R] * (1.0 / acc[R : R + 1]))
         return parts
 
-    parts = lift_local(2, emitted(2))
+    first = emitted(2)
+    q1f[...] = emitted(1)
+    upart[...] = emitted(0)
+    parts = lift_local(2, first)
     for n, part in enumerate(parts):
         m2[:, n * NB : (n + 1) * NB] = part
-    parts = lift_local(1, emitted(1) * jnp.where(chain, m2[...], 1.0))
+    parts = lift_local(1, q1f[...] * jnp.where(chain, m2[...], 1.0))
     for n, part in enumerate(parts):
         cols = slice(n * NB, (n + 1) * NB)
-        upart[:, cols] = part * jnp.where(chain, 1.0, m2[:, cols])
-    upart[...] = upart[...] * emitted(0)
+        upart[:, cols] = upart[:, cols] * part * jnp.where(chain, 1.0, m2[:, cols])
     loads["m", 0].wait()
 
     pl.semaphore_wait(barrier, lvl + (groups - 1) + jnp.where(is_root, 0, 1))
@@ -337,10 +339,18 @@
 
     @pl.when(lvl == 0)
     def _():
-        for n, part in enumerate(lift_local(0, upart[...])):
-            m_out[:, n * NB : (n + 1) * NB] = part.astype(BF16)
-        for i in range(C):
-            up_start(i)
+        for n in range(2):
+            part = slice(n * half, (n + 1) * half)
+            lam = scaled(upart[part, :])
+            lam_all[0, part_of(0, n), :] = lam
+            left = jnp.concatenate([lam, ones], axis=0)
+            for b in range(K // NB):
+                cols = slice(b * NB, (b + 1) * NB)
+                acc = dot_nt(left, A[0, cols, :])
+                macc[0, part, cols] = acc[:half]
+                m_out[part, cols] = (acc[:half] * (1.0 / acc[half : half + 1])).astype(BF16)
+            for i in range(n * C // 2, (n + 1) * C // 2):
+                up_start(i)
         ag_copy(0, 1).start()
         ag_copy(0, groups - 1).start()
         aux()
@@ -351,6 +361,7 @@
         aux()
         for b in range(K // NB):
             A0T[:, b * NB : (b + 1) * NB] = A[0, b * NB : (b + 1) * NB, :].T
+        inv_row[...] = 1.0 / dot_nn(ones, A0T[...])[:8]
 
     def early_child(j, carry):
         arrived(msg_in.at[j], early_recv.at[j])
@@ -370,27 +381,26 @@
         for n in range(m):
             arrived(msg_in.at[lvl - 1, chunk(i + n)], up_recv.at[i + n])
         lam = scaled(upart[rows, :] * msg_in[lvl - 1, rows, :].astype(F32))
-        acc = dot_nn(jnp.concatenate([lam, ones], axis=0), A0T[...])
-        inverse = 1.0 / acc[M : M + 1]
+        acc = dot_nn(lam, A0T[...])
         if m == 1:
-            m_out[rows, :] = (acc[:M] * inverse).astype(BF16)
+            m_out[rows, :] = (acc * inv_row[0:1, :]).astype(BF16)
             up_start(i)
-            macc[0, rows, :] = 1.0 / acc[:M]
+            macc[0, rows, :] = 1.0 / acc
         else:
-            inv_row[0:1, :] = inverse
-            macc[0, rows, :] = acc[:M]
+            macc[0, rows, :] = acc
         lam_all[0, pl.ds(pl.multiple_of(own + i * S, S), M), :] = lam
 
     at_once = [(0, lvl > 1)]
     if levels > 4:
         at_once.append((3, lvl > 4))
 
-    def down(i, m=1):
+    def down(i, m=1, root=False):
         M = m * S
         row = pl.multiple_of(i * S, S)
         rows = pl.ds(row, M)
-        if m == 1:
-            arrived(q_in.at[rows], dn_recv.at[i])
+        if not root:
+            for n in range(m):
+                arrived(q_in.at[chunk(i + n)], dn_recv.at[i + n])
             left = (q_in[rows, :].astype(F32) * macc[0, rows, :]).astype(BF16)
         else:
             weight = (prior[...] / jnp.sum(prior[...], axis=1, keepdims=True)) * inv_row[0:1, :]
@@ -401,7 +411,7 @@
         there = pl.ds(pl.multiple_of(own + row, S), M)
         q = lam_all[0, there, :].astype(F32) * dot_nn(left, A[0])
         qb[0, rows, :] = q.astype(BF16)
-        for n in range(m):
+        for n in range(m if m == 1 or root else 0):
 
             @pl.when(lvl > 0)
             def _():
@@ -413,7 +423,7 @@
                 def _(j=j):
                     dn_start(j, 2**j, i + n)
 
-        if m > 1 and levels > 5:
+        if root and levels > 5:
             for n in range(m):
                 dn_start(4, 16, i + n)
         q0f[rows, :] = q
@@ -468,9 +478,9 @@
     @pl.when(is_root)
     def _():
         up(0, C // 2)
-        down(0, C // 2)
+        down(0, C // 2, True)
         up(C // 2, C // 2)
-        down(C // 2, C // 2)
+        down(C // 2, C // 2, True)
         gather_first()
 
     def step(s, carry):
@@ -492,13 +502,19 @@
         def _():
             up(s)
 
-        @pl.when(s >= C)
+        @pl.when(jnp.logical_and(s >= C, lvl > 0))
         def _():
             down(s - C)
 
-            @pl.when(jnp.logical_and(s == C + C // 2 - 1, lvl <= 1))
+            @pl.when(jnp.logical_and(s == C + C // 2 - 1, lvl == 1))
             def _():
                 settle_both(0)
+
+        @pl.when(jnp.logical_and(s == C, lvl == 0))
+        def _():
+            down(0, C // 2)
+            settle_both(0)
+            down(C // 2, C // 2)
 
         return carry
 

time: 69.1 us -> 67.1 us (0.971)
  the two profiles are of different devices: /device:TPU:59 before, /device:TPU:57 now
where the time goes in v4:
time: 67.1 us; the launch traced here: 67 us
  Pallas kernels  66.3 us (99%)
    pallas_call x1, Pallas kernels, per_device(): pl.pallas_call(functools.partial(kernel, levels, groups), out_shape=resul...  65.1 us

profile of v4, /device:TPU:57, one launch (start us, length us, event | category | flops | bytes accessed | tf_op | source)
XLA Modules:
  0.0 67.0 jit_solution(5973788657785986439)
XLA Ops:
  0.6 65.1 %tree_pass.1 = (bf16[3,256,1024]{2,1,0:T(8,128)(2,1)S(1)}, bf16[3,256,256]{2,1,0:T(8,128)(2,1)S(1)}) custom-call(bf16[3,1024,1024]{2,1,0:T(8,128)(2,1)} %mixing.1, bf16[3,256,1024]{2,1,0:T(8,128)(2,1)} %emission.1, f32[1,1024]{1,0:T(1,128)} %bitcast.1, s32[3]{0:T(128)} %parent.1, s32[3,128]{1,0:T(4,128)} %observed.1), custom_call_target="tpu_custom_call" | custom-call | flops 1000000000 | bytes 10000000 | tf_op jit(solution)/shard_map/tree_pass/pallas_call | solution.py:654
  65.7 1.3 %store_counts.1 = (bf16[3,256,1024]{2,1,0:T(8,128)(2,1)}, bf16[3,256,256]{2,1,0:T(8,128)(2,1)}) custom-call(bf16[3,256,1024]{2,1,0:T(8,128)(2,1)S(1)} %get-tuple-element.4.pair_v, bf16[3,256,256]{2,1,0:T(8,128)(2,1)S(1)} %get-tuple-element.5.emit_v), custom_call_target="tpu_custom_call" | custom-call | tf_op jit(solution)/shard_map/store_counts/pallas_call | solution.py:713

commit v5 on v4

--- a/solution.py
+++ b/solution.py
@@ -393,6 +393,10 @@
     at_once = [(0, lvl > 1)]
     if levels > 4:
         at_once.append((3, lvl > 4))
+    if levels > 3:
+        at_once.append((2, lvl > 3))
+    if levels > 2:
+        at_once.append((1, lvl == 3))
 
     def down(i, m=1, root=False):
         M = m * S
@@ -477,10 +481,9 @@
 
     @pl.when(is_root)
     def _():
-        up(0, C // 2)
-        down(0, C // 2, True)
-        up(C // 2, C // 2)
-        down(C // 2, C // 2, True)
+        for b in range(4):
+            up(b * C // 4, C // 4)
+            down(b * C // 4, C // 4, True)
         gather_first()
 
     def step(s, carry):
@@ -521,10 +524,8 @@
     lax.fori_loop(jnp.where(lvl == 0, C, 0), jnp.where(is_root, 0, 2 * C), step, 0)
 
     later = []
-    if levels > 3:
-        later.append((2, lvl > 3))
     if levels > 2:
-        later.append((1, lvl > 2))
+        later.append((1, lvl > 3))
     for j, test in later:
 
         @pl.when(test)

time: 67.1 us -> 66.1 us (0.985)
  the two profiles are of different devices: /device:TPU:57 before, /device:TPU:249 now
where the time goes in v5:
time: 66.1 us; the launch traced here: 65.4 us
  Pallas kernels  64.6 us (98%)
  between operations  0.8 us (1%)
    pallas_call x1, Pallas kernels, per_device(): pl.pallas_call(functools.partial(kernel, levels, groups), out_shape=resul...  63.3 us

profile of v5, /device:TPU:249, one launch (start us, length us, event | category | flops | bytes accessed | tf_op | source)
XLA Modules:
  0.0 65.4 jit_solution(16219641016698739219)
XLA Ops:
  0.6 63.3 %tree_pass.1 = (bf16[3,256,1024]{2,1,0:T(8,128)(2,1)S(1)}, bf16[3,256,256]{2,1,0:T(8,128)(2,1)S(1)}) custom-call(bf16[3,1024,1024]{2,1,0:T(8,128)(2,1)} %mixing.1, bf16[3,256,1024]{2,1,0:T(8,128)(2,1)} %emission.1, f32[1,1024]{1,0:T(1,128)} %bitcast.1, s32[3]{0:T(128)} %parent.1, s32[3,128]{1,0:T(4,128)} %observed.1), custom_call_target="tpu_custom_call" | custom-call | flops 1000000000 | bytes 10000000 | tf_op jit(solution)/shard_map/tree_pass/pallas_call | solution.py:655
  63.9 1.3 %store_counts.1 = (bf16[3,256,1024]{2,1,0:T(8,128)(2,1)}, bf16[3,256,256]{2,1,0:T(8,128)(2,1)}) custom-call(bf16[3,256,1024]{2,1,0:T(8,128)(2,1)S(1)} %get-tuple-element.4.pair_v, bf16[3,256,256]{2,1,0:T(8,128)(2,1)S(1)} %get-tuple-element.5.emit_v), custom_call_target="tpu_custom_call" | custom-call | tf_op jit(solution)/shard_map/store_counts/pallas_call | solution.py:714
